TPU v7x, 256 devices: a whole 4x4x8 slice. The times are simulated.
256 devices in a mesh: dp: 64 (over z, y, x_hi), strip: 4 (over x_lo, core).
Axes of the slice: x: 4 (x_hi: 2, x_lo: 2; x = x_hi * 2 + x_lo), y: 4, z: 8, core: 2. Of those that a mesh axis runs over, the one named last changes fastest.
Arguments:
- images: bfloat16 [256, 3, 32, 128], P('dp', None, 'strip'), may hold values from -16 to 16
- perturbation: float32 [3, 32, 128], P(None, 'strip'), may hold values from -0.5 to 0.5
- labels: int32 [256], P(('dp', 'strip')), may hold values from 0 to 61
- step_levels: int32 [3], replicated, may hold values from 1 to 4
- stem_weight: bfloat16 [48, 192], replicated, may hold values from -0.875 to 0.875
- stem_gain: float32 [192], replicated, may hold values from 0.25 to 1.75
- dw1_kernel: bfloat16 [49, 192], replicated, may hold values from -0.875 to 0.875
- norm1_gain: float32 [192], replicated, may hold values from 0.25 to 1.75
- up1_weight: bfloat16 [192, 768], replicated, may hold values from -0.4375 to 0.4375
- down1_weight: bfloat16 [768, 192], replicated, may hold values from -0.21875 to 0.21875
- scale1: float32 [192], replicated, may hold values from 0.3 to 1
- down_gain: float32 [192], replicated, may hold values from 0.25 to 1.75
- ds_weight: bfloat16 [768, 384], replicated, may hold values from -0.21875 to 0.21875
- head_gain: float32 [384], replicated, may hold values from 0.25 to 1.75
- head_weight: bfloat16 [384, 62], replicated, may hold values from -0.3125 to 0.3125
Outputs:
- new_perturbation: float32 [3, 32, 128], P(None, 'strip')
- losses: float32 [256], P(('dp', 'strip'))
- stem_grad: float32 [48, 192], P(None, 'dp')
- dw1_grad: float32 [49, 192], P(None, 'dp')
- up1_grad: float32 [192, 768], P(None, 'dp')
- down1_grad: float32 [768, 192], P('dp')
- ds_grad: float32 [768, 384], P(None, 'dp')
- head_grad: float32 [384, 62], P('dp')
All inputs are finite; a program needn't handle non-finite values.
Results may differ from a plain program's by a relative error of at most 0.013.
Values may be sent and summed in bfloat16 or wider, within the bound.
A program may use at most 64 MiB of HBM per device.

v0:
```python
import jax
import jax.numpy as jnp
from jax import lax
from jax.sharding import PartitionSpec as P

KS = 7
PATCH = 4


EPS_NORM = 1e-06
EPS_ROOT = 1e-12
BOUND = 0.5
STEP_UNIT = 0.1


def norm_gain(values_in, gain_vec):
    centre = jnp.mean(values_in, axis=-1, keepdims=True)
    centred = values_in - centre
    spread = jnp.mean(centred * centred, axis=-1, keepdims=True)
    return centred * lax.rsqrt(spread + EPS_NORM) * gain_vec


def norm_back(values_in, gain_vec, grad_out):

    def apply_norm(argument):
        return norm_gain(argument, gain_vec)

    return jax.vjp(apply_norm, values_in)[1](grad_out)[0]


def dense(values_in, weight):
    flattened = values_in.astype(jnp.bfloat16).reshape(-1, values_in.shape[-1])
    result = jnp.dot(flattened, weight, preferred_element_type=jnp.float32)
    return result.reshape(values_in.shape[:-1] + (weight.shape[1],))


def dense_back(grad_out, values_in, weight):
    grads_low = grad_out.astype(jnp.bfloat16).reshape(-1, grad_out.shape[-1])
    inputs_low = values_in.astype(jnp.bfloat16).reshape(-1, values_in.shape[-1])
    grad_in = jnp.dot(grads_low, weight.T, preferred_element_type=jnp.float32)
    grad_weight = jnp.dot(inputs_low.T, grads_low, preferred_element_type=jnp.float32)
    return (grad_in.reshape(values_in.shape), grad_weight)


def gelu_exact(values_in):
    return jax.nn.gelu(values_in, approximate=False)


def gelu_back(values_in, grad_out):
    return jax.vjp(gelu_exact, values_in)[1](grad_out)[0]


def depthwise(padded, kernel):
    channels = kernel.shape[1]
    taps = kernel.reshape(KS, KS, 1, channels)
    return lax.conv_general_dilated(
        padded,
        taps,
        (1, 1),
        "VALID",
        dimension_numbers=("NHWC", "HWIO", "NHWC"),
        feature_group_count=channels,
        precision=lax.Precision.HIGHEST,
    )


def flipped(kernel):
    channels = kernel.shape[1]
    return kernel.reshape(KS, KS, channels)[::-1, ::-1].reshape(KS * KS, channels)


def kernel_back(padded, kernel, grad_out):

    def apply_taps(argument):
        return depthwise(padded, argument)

    return jax.vjp(apply_taps, kernel)[1](grad_out)[0]


def pad_both(values_in):
    half = KS // 2
    return jnp.pad(values_in, ((0, 0), (half, half), (half, half), (0, 0)))


def patchify(pixels):
    number, channels, row_count, col_count = pixels.shape
    blocks = pixels.reshape(number, channels, row_count // PATCH, PATCH, col_count // PATCH, PATCH)
    return blocks.transpose(0, 2, 4, 1, 3, 5).reshape(
        number, row_count // PATCH, col_count // PATCH, channels * PATCH * PATCH
    )


def unpatchify(grads_in, channels):
    number, row_count, col_count, _ = grads_in.shape
    blocks = grads_in.reshape(number, row_count, col_count, channels, PATCH, PATCH)
    return blocks.transpose(0, 3, 1, 4, 2, 5).reshape(
        number, channels, row_count * PATCH, col_count * PATCH
    )


def merge_pairs(values_in):
    number, row_count, col_count, channels = values_in.shape
    blocks = values_in.reshape(number, row_count // 2, 2, col_count // 2, 2, channels)
    return blocks.transpose(0, 1, 3, 2, 4, 5).reshape(
        number, row_count // 2, col_count // 2, 4 * channels
    )


def split_pairs(grads_in, channels):
    number, row_count, col_count, _ = grads_in.shape
    blocks = grads_in.reshape(number, row_count, col_count, 2, 2, channels)
    return blocks.transpose(0, 1, 3, 2, 4, 5).reshape(
        number, row_count * 2, col_count * 2, channels
    )


def block_forward(inputs, padded, kernel, gain_vec, w_up, w_down, layer_scale):
    mixed_out = depthwise(padded, kernel)
    normed = norm_gain(mixed_out, gain_vec)
    upper_in = dense(normed, w_up)
    hidden = gelu_exact(upper_in)
    branch = dense(hidden, w_down)
    return (inputs + layer_scale * branch, (mixed_out, normed, upper_in, hidden))


def block_backward(grad_out, padded, kernel, gain_vec, w_up, w_down, layer_scale, stored):
    mixed_out, normed, upper_in, hidden = stored
    grad_branch = grad_out * layer_scale
    grad_hidden, grad_down = dense_back(grad_branch, hidden, w_down)
    grad_upper = gelu_back(upper_in, grad_hidden)
    grad_normed, grad_up = dense_back(grad_upper, normed, w_up)
    grad_mixed = norm_back(mixed_out, gain_vec, grad_normed)
    grad_kernel = kernel_back(padded, kernel, grad_mixed)
    return (grad_mixed, grad_kernel, grad_up, grad_down)


def section_two(held, labels, down_gain, ds_weight, head_gain, head_weight):
    source = held.astype(jnp.float32)
    normed_in = norm_gain(source, down_gain)
    merged = merge_pairs(normed_in)
    start_two = dense(merged, ds_weight)
    pooled = jnp.mean(start_two, axis=(1, 2))
    head_in = norm_gain(pooled, head_gain)
    logits = dense(head_in, head_weight)
    onehot = (labels[:, None] == lax.iota(jnp.int32, logits.shape[1])[None, :]).astype(jnp.float32)
    losses = jax.nn.logsumexp(logits, axis=1) - jnp.sum(onehot * logits, axis=1)
    grad_logits = jax.nn.softmax(logits, axis=1) - onehot
    grad_head_in, grad_head = dense_back(grad_logits, head_in, head_weight)
    grad_pooled = norm_back(pooled, head_gain, grad_head_in)
    cells = start_two.shape[1] * start_two.shape[2]
    grad_start = jnp.broadcast_to((grad_pooled / cells)[:, None, None, :], start_two.shape)
    grad_merged, grad_ds = dense_back(grad_start, merged, ds_weight)
    grad_normed_in = split_pairs(grad_merged, source.shape[3])
    grad_source = norm_back(source, down_gain, grad_normed_in)
    grad_held = lax.optimization_barrier(grad_source.astype(jnp.bfloat16))
    return (losses, grad_held, (grad_ds, grad_head))


def on_device(
    images,
    perturbation,
    labels,
    step_levels,
    stem_weight,
    stem_gain,
    dw1_kernel,
    norm1_gain,
    up1_weight,
    down1_weight,
    scale1,
    down_gain,
    ds_weight,
    head_gain,
    head_weight,
):
    kernel_one = dw1_kernel.astype(jnp.float32)
    pixels = lax.all_to_all(images, "strip", split_axis=0, concat_axis=2, tiled=True)
    whole_delta = lax.all_gather(perturbation, "strip", axis=1, tiled=True)
    perturbed = pixels.astype(jnp.float32) + whole_delta[None]
    patches = patchify(perturbed)
    stem_pre = dense(patches, stem_weight)
    stem_out = lax.optimization_barrier(norm_gain(stem_pre, stem_gain).astype(jnp.bfloat16))
    padded_one = pad_both(stem_out).astype(jnp.float32)
    block_out, stored_one = block_forward(
        stem_out.astype(jnp.float32),
        padded_one,
        kernel_one,
        norm1_gain,
        up1_weight,
        down1_weight,
        scale1,
    )
    section_out = lax.optimization_barrier(block_out.astype(jnp.bfloat16))
    losses, grad_held, grads_two = section_two(
        section_out, labels, down_gain, ds_weight, head_gain, head_weight
    )
    grad_block = grad_held.astype(jnp.float32)
    grad_mixed, grad_dw1, grad_up1, grad_down1 = block_backward(
        grad_block, padded_one, kernel_one, norm1_gain, up1_weight, down1_weight, scale1, stored_one
    )
    grad_stem = grad_block + depthwise(pad_both(grad_mixed), flipped(kernel_one))
    grad_pre = norm_back(stem_pre, stem_gain, grad_stem)
    grad_patches, grad_stem_weight = dense_back(grad_pre, patches, stem_weight)
    grad_pixels = unpatchify(grad_patches, 3)
    delta_part = lax.psum_scatter(
        jnp.sum(grad_pixels, axis=0).astype(jnp.bfloat16), "strip", scatter_dimension=1, tiled=True
    ).astype(jnp.float32)
    grad_ds, grad_head = grads_two
    shares = (
        lax.psum_scatter(grad_stem_weight, "dp", scatter_dimension=1, tiled=True),
        lax.psum_scatter(grad_dw1, "dp", scatter_dimension=1, tiled=True),
        lax.psum_scatter(grad_up1, "dp", scatter_dimension=1, tiled=True),
        lax.psum_scatter(grad_down1, "dp", scatter_dimension=0, tiled=True),
        lax.psum_scatter(grad_ds, "dp", scatter_dimension=1, tiled=True),
        lax.psum_scatter(grad_head, "dp", scatter_dimension=0, tiled=True),
    )
    summed = (
        lax.psum(shares[0].astype(jnp.bfloat16), "strip").astype(jnp.float32),
        lax.psum(shares[1].astype(jnp.bfloat16), "strip").astype(jnp.float32),
        lax.psum(shares[2].astype(jnp.bfloat16), "strip").astype(jnp.float32),
        lax.psum(shares[3].astype(jnp.bfloat16), "strip").astype(jnp.float32),
        lax.psum(shares[4].astype(jnp.bfloat16), "strip").astype(jnp.float32),
        lax.psum(shares[5].astype(jnp.bfloat16), "strip").astype(jnp.float32),
    )
    stem_grad, dw1_grad, up1_grad, down1_grad, ds_grad, head_grad = summed
    levels = STEP_UNIT * step_levels.astype(jnp.float32)
    summed_delta = lax.psum(delta_part, "dp")
    squares = lax.psum(jnp.sum(summed_delta * summed_delta), "strip")
    cells = delta_part.size * lax.axis_size("strip")
    spread = jnp.sqrt(squares / cells + EPS_ROOT)
    new_perturbation = jnp.clip(
        perturbation + levels[:, None, None] * summed_delta / spread, -BOUND, BOUND
    )
    return (new_perturbation, losses, stem_grad, dw1_grad, up1_grad, down1_grad, ds_grad, head_grad)


def solution(mesh):
    return jax.shard_map(
        on_device,
        mesh=mesh,
        in_specs=(
            P("dp", None, "strip", None),
            P(None, "strip", None),
            P(("dp", "strip")),
            P(),
            P(),
            P(),
            P(),
            P(),
            P(),
            P(),
            P(),
            P(),
            P(),
            P(),
            P(),
        ),
        out_specs=(
            P(None, "strip", None),
            P(("dp", "strip")),
            P(None, "dp"),
            P(None, "dp"),
            P(None, "dp"),
            P("dp", None),
            P(None, "dp"),
            P("dp", None),
        ),
        check_vma=False,
    )
```

profile of v0, /device:TPU:1, one launch (start us, length us, event | category | flops | bytes accessed | tf_op | source)
XLA Modules:
  0.0 820.2 jit_solution(3639042860239779611)
XLA Ops:
  0.6 6.6 all-to-all-start
  18.1 5.4 all_gather.3
  23.5 1.7 convert_element_type.200
  26.8 4.8 fusion.63
  33.1 2.8 multiply_convert_fusion
  43.9 1.8 fusion.53
  53.9 180.5 %fusion.51 = (f32[192,16]{0,1:T(8,128)S(1)}, f32[16,192]{1,0:T(8,128)S(1)}, f32[768,8]{0,1:T(8,128)S(1)}) fusion(f32[192,768]{0,1:T(8,128)S(1)} %convolution_bitcast_fusion.2, f32[768,192]{1,0:T(8,128)} %convolution_bitcast_fusion.1, f32[768,384]{0,1:T(8,128)S(1)} %convolution_bitcast_fusion), kind=kCustom, calls=%all-reduce-scatter.3 | all-reduce-scatter fusion | flops 786434 | bytes 2409472
  234.5 1.4 collective-permute-start.14
  237.2 1.5 collective-permute-start.12
  241.2 9.7 %convolution_reduce_fusion = f32[7,7,192]{2,1,0:T(8,128)S(1)} fusion(bf16[1,8,32,192]{3,2,1,0:T(8,128)(2,1)S(1)} %copy-done.6, f32[1,8,32,192]{3,0,2,1:T(1,128)S(1)} %get-tuple-element.32, f32[8,32]{1,0:T(8,128)S(1)} %negate_multiply_fusion.2), kind=kOutput, calls=%fused_computation.13 | convolution fusion | flops 21540864 | bytes 333568 | tf_op jit(solution)/shard_map/transpose(jvp())/conv_general_dilated | solution.py:56
  250.9 1.6 fusion.31
  256.1 5.3 collective-permute-start.15
  261.4 3.8 collective-permute-start.31
  265.3 35.9 %all-reduce = bf16[3,32,128]{2,1,0:T(8,128)(2,1)S(1)} all-reduce(bf16[3,32,128]{2,1,0:T(8,128)(2,1)S(1)} %convert_element_type.225), channel_id=2, replica_groups=mesh['dp'=64,'strip'=4] {'strip'}, use_global_device_ids=true, to_apply=%region_19.20.clone | all-reduce | flops 12288 | bytes 49152
  303.9 9.0 %collective-permute-start.9 = (bf16[192,16]{0,1:T(8,128)(2,1)S(1)}, bf16[192,16]{0,1:T(8,128)(2,1)S(1)}, u32[]{:S(2)}, u32[]{:S(2)}) collective-permute-start(bf16[192,16]{0,1:T(8,128)(2,1)S(1)} %convert.108), channel_id=1, source_target_pairs={{0,40},{4,44},{8,48},{12,52},{16,56},{20,60},{24,64},{28,68},{32,7... | collective-permute-start | bytes 18440
  313.0 2.3 collective-permute-start.8
  316.6 6.1 collective-permute-start.6
  324.1 2.8 collective-permute-start.4
  326.9 300.7 %all-reduce.14 = (f32[3,8,128]{2,1,0:T(8,128)S(1)}, bf16[48,192]{0,1:T(8,128)(2,1)S(1)}, bf16[49,192]{0,1:T(8,128)(2,1)S(1)}, bf16[384,62]{1,0:T(8,128)(2,1)S(1)}) all-reduce(f32[3,8,128]{2,1,0:T(8,128)S(1)} %dynamic-slice_convert_fusion.3, f32[48,192]{0,1:T(8,128)S(1)} %convolution_bitcast_fusion.4, ...), channel_id=1, replica_groups=mesh['dp'=64,'strip'=4] {'dp'}, use_global_device_ids=true, to_apply=%region_20.21 | all-reduce | flops 45504 | bytes 279168 | tf_op jit(solution)/shard_map/psum | solution.py:227
  634.7 61.9 %psum.57 = f32[]{:T(128)} all-reduce(f32[]{:T(128)} %multiply_reduce_fusion.3), channel_id=1, replica_groups=mesh['dp'=64,'strip'=4] {'strip'}, use_global_device_ids=true, to_apply=%region_22.23 | all-reduce | flops 1 | bytes 8 | tf_op jit(solution)/shard_map/psum | solution.py:228
  697.4 9.6 %collective-permute-start.29 = (bf16[16,192]{1,0:T(8,128)(2,1)S(1)}, bf16[16,192]{1,0:T(8,128)(2,1)S(1)}, u32[]{:S(2)}, u32[]{:S(2)}) collective-permute-start(bf16[16,192]{1,0:T(8,128)(2,1)S(1)} %convert.107), channel_id=1, source_target_pairs={{0,56},{4,60},{8,64},{12,68},{16,72},{20,76},{24,80},{28,84},{32,8... | collective-permute-start | bytes 18440
  707.0 3.4 collective-permute-start.28
  710.5 11.3 %collective-permute-start.27 = (bf16[16,192]{1,0:T(8,128)(2,1)S(1)}, bf16[16,192]{1,0:T(8,128)(2,1)S(1)}, u32[]{:S(2)}, u32[]{:S(2)}) collective-permute-start(bf16[16,192]{1,0:T(8,128)(2,1)S(1)} %convert.107), channel_id=1, source_target_pairs={{0,48},{4,52},{8,56},{12,60},{16,64},{20,68},{24,72},{28,76},{32,8... | collective-permute-start | bytes 18440
  721.8 2.5 collective-permute-start.26
  726.3 2.6 collective-permute-start.24
  728.9 3.1 collective-permute-start.23
  732.0 4.0 collective-permute-start.22
  736.0 2.2 collective-permute-start.21
  738.2 2.8 collective-permute-start.20
  741.1 3.4 collective-permute-start.19
  744.5 2.2 collective-permute-start.18
  746.7 2.6 collective-permute-start.17
  749.3 4.3 collective-permute-start.16
  754.9 2.0 collective-permute-start.46
  758.3 2.5 collective-permute-start.44
  760.7 2.0 collective-permute-start.43
  765.4 1.9 concatenate
  767.3 1.7 collective-permute-start.41
  769.0 3.4 collective-permute-start.40
  773.7 4.3 collective-permute-start.38
  779.4 1.9 concatenate.1
  781.3 2.6 collective-permute-start.36
  783.9 3.2 collective-permute-start.35
  787.1 2.5 collective-permute-start.34
  789.6 2.8 collective-permute-start.33
  792.4 3.7 collective-permute-start.32
  797.0 1.8 concatenate.2
  798.8 16.7 %all-reduce.11 = (bf16[48,3]{0,1:T(4,128)(2,1)S(1)}, bf16[49,3]{0,1:T(4,128)(2,1)S(1)}, bf16[192,12]{0,1:T(8,128)(2,1)S(1)}, bf16[12,192]{1,0:T(8,128)(2,1)S(1)}...) all-reduce(bf16[48,3]{0,1:T(4,128)(2,1)S(1)} %dynamic-slice_convert, ...), channel_id=1, replica_groups=mesh['dp'=64,'strip'=4] {'strip'}, use_global_device_ids=true, to_apply=%region_26.27 | all-reduce | flops 9879 | bytes 39516 | tf_op jit(solution)/shard_map/psum | solution.py:218
  (229 shorter events, 54.4 us)
Async XLA Ops:
  0.6 22.8 %all-to-all-start = ((bf16[4,3,8,128]{3,2,1,0:T(8,128)(2,1)}), bf16[4,3,8,128]{3,2,1,0:T(8,128)(2,1)S(1)}, u32[]{:S(2)}, u32[]{:S(2)}) async-start(bf16[4,3,8,128]{3,2,1,0:T(8,128)(2,1)} %param.15), calls=%async_computation | async-start | bytes 49152 | tf_op jit(solution)/shard_map/all_to_all | solution.py:177
  234.5 69.4 %collective-permute-start.14 = (bf16[192,16]{0,1:T(8,128)(2,1)S(1)}, bf16[192,16]{0,1:T(8,128)(2,1)S(1)}, u32[]{:S(2)}, u32[]{:S(2)}) collective-permute-start(bf16[192,16]{0,1:T(8,128)(2,1)S(1)} %convert.108), channel_id=1, source_target_pairs={{0,60},{4,64},{8,68},{12,72},{16,76},{20,80},{24,84},{28,88},{32,9... | collective-permute-start | bytes 18440
  235.9 77.1 %collective-permute-start.13 = (bf16[192,16]{0,1:T(8,128)(2,1)S(1)}, bf16[192,16]{0,1:T(8,128)(2,1)S(1)}, u32[]{:S(2)}, u32[]{:S(2)}) collective-permute-start(bf16[192,16]{0,1:T(8,128)(2,1)S(1)} %convert.108), channel_id=1, source_target_pairs={{0,56},{4,60},{8,64},{12,68},{16,72},{20,76},{24,80},{28,84},{32,8... | collective-permute-start | bytes 18440
  237.2 78.1 %collective-permute-start.12 = (bf16[192,16]{0,1:T(8,128)(2,1)S(1)}, bf16[192,16]{0,1:T(8,128)(2,1)S(1)}, u32[]{:S(2)}, u32[]{:S(2)}) collective-permute-start(bf16[192,16]{0,1:T(8,128)(2,1)S(1)} %convert.108), channel_id=1, source_target_pairs={{0,52},{4,56},{8,60},{12,64},{16,68},{20,72},{24,76},{28,80},{32,8... | collective-permute-start | bytes 18440
  256.1 45.1 %collective-permute-start.15 = (bf16[192,12]{0,1:T(8,128)(2,1)S(1)}, bf16[192,12]{0,1:T(8,128)(2,1)S(1)}, u32[]{:S(2)}, u32[]{:S(2)}) collective-permute-start(bf16[192,12]{0,1:T(8,128)(2,1)S(1)} %slice), channel_id=1, source_target_pairs={{0,64},{4,68},{8,72},{12,76},{16,80},{20,84},{24,88},{28,92},{32,9... | collective-permute-start | bytes 13832
  261.4 41.1 %collective-permute-start.31 = (bf16[12,192]{1,0:T(8,128)(2,1)S(1)}, bf16[12,192]{1,0:T(8,128)(2,1)S(1)}, u32[]{:S(2)}, u32[]{:S(2)}) collective-permute-start(bf16[12,192]{1,0:T(8,128)(2,1)S(1)} %slice.1), channel_id=1, source_target_pairs={{0,64},{4,68},{8,72},{12,76},{16,80},{20,84},{24,88},{28,92},{32,9... | collective-permute-start | bytes 13832
  301.2 15.4 %collective-permute-start.11 = (bf16[192,16]{0,1:T(8,128)(2,1)S(1)}, bf16[192,16]{0,1:T(8,128)(2,1)S(1)}, u32[]{:S(2)}, u32[]{:S(2)}) collective-permute-start(bf16[192,16]{0,1:T(8,128)(2,1)S(1)} %convert.108), channel_id=1, source_target_pairs={{0,48},{4,52},{8,56},{12,60},{16,64},{20,68},{24,72},{28,76},{32,8... | collective-permute-start | bytes 18440
  302.5 20.2 %collective-permute-start.10 = (bf16[192,16]{0,1:T(8,128)(2,1)S(1)}, bf16[192,16]{0,1:T(8,128)(2,1)S(1)}, u32[]{:S(2)}, u32[]{:S(2)}) collective-permute-start(bf16[192,16]{0,1:T(8,128)(2,1)S(1)} %convert.108), channel_id=1, source_target_pairs={{0,44},{4,48},{8,52},{12,56},{16,60},{20,64},{24,68},{28,72},{32,7... | collective-permute-start | bytes 18440
  303.9 20.2 %collective-permute-start.9 = (bf16[192,16]{0,1:T(8,128)(2,1)S(1)}, bf16[192,16]{0,1:T(8,128)(2,1)S(1)}, u32[]{:S(2)}, u32[]{:S(2)}) collective-permute-start(bf16[192,16]{0,1:T(8,128)(2,1)S(1)} %convert.108), channel_id=1, source_target_pairs={{0,40},{4,44},{8,48},{12,52},{16,56},{20,60},{24,64},{28,68},{32,7... | collective-permute-start | bytes 18440
  313.0 314.5 %collective-permute-start.8 = (bf16[192,16]{0,1:T(8,128)(2,1)S(1)}, bf16[192,16]{0,1:T(8,128)(2,1)S(1)}, u32[]{:S(2)}, u32[]{:S(2)}) collective-permute-start(bf16[192,16]{0,1:T(8,128)(2,1)S(1)} %convert.108), channel_id=1, source_target_pairs={{0,36},{4,40},{8,44},{12,48},{16,52},{20,56},{24,60},{28,64},{32,6... | collective-permute-start | bytes 18440
  315.3 313.6 %collective-permute-start.7 = (bf16[192,16]{0,1:T(8,128)(2,1)S(1)}, bf16[192,16]{0,1:T(8,128)(2,1)S(1)}, u32[]{:S(2)}, u32[]{:S(2)}) collective-permute-start(bf16[192,16]{0,1:T(8,128)(2,1)S(1)} %convert.108), channel_id=1, source_target_pairs={{0,32},{4,36},{8,40},{12,44},{16,48},{20,52},{24,56},{28,60},{32,6... | collective-permute-start | bytes 18440
  316.6 313.6 %collective-permute-start.6 = (bf16[192,16]{0,1:T(8,128)(2,1)S(1)}, bf16[192,16]{0,1:T(8,128)(2,1)S(1)}, u32[]{:S(2)}, u32[]{:S(2)}) collective-permute-start(bf16[192,16]{0,1:T(8,128)(2,1)S(1)} %convert.108), channel_id=1, source_target_pairs={{0,28},{4,32},{8,36},{12,40},{16,44},{20,48},{24,52},{28,56},{32,6... | collective-permute-start | bytes 18440
  322.8 308.7 %collective-permute-start.5 = (bf16[192,16]{0,1:T(8,128)(2,1)S(1)}, bf16[192,16]{0,1:T(8,128)(2,1)S(1)}, u32[]{:S(2)}, u32[]{:S(2)}) collective-permute-start(bf16[192,16]{0,1:T(8,128)(2,1)S(1)} %convert.108), channel_id=1, source_target_pairs={{0,24},{4,28},{8,32},{12,36},{16,40},{20,44},{24,48},{28,52},{32,5... | collective-permute-start | bytes 18440
  324.1 308.7 %collective-permute-start.4 = (bf16[192,16]{0,1:T(8,128)(2,1)S(1)}, bf16[192,16]{0,1:T(8,128)(2,1)S(1)}, u32[]{:S(2)}, u32[]{:S(2)}) collective-permute-start(bf16[192,16]{0,1:T(8,128)(2,1)S(1)} %convert.108), channel_id=1, source_target_pairs={{0,20},{4,24},{8,28},{12,32},{16,36},{20,40},{24,44},{28,48},{32,5... | collective-permute-start | bytes 18440
  627.6 69.8 %collective-permute-start.3 = (bf16[192,16]{0,1:T(8,128)(2,1)S(1)}, bf16[192,16]{0,1:T(8,128)(2,1)S(1)}, u32[]{:S(2)}, u32[]{:S(2)}) collective-permute-start(bf16[192,16]{0,1:T(8,128)(2,1)S(1)} %convert.108), channel_id=1, source_target_pairs={{0,16},{4,20},{8,24},{12,28},{16,32},{20,36},{24,40},{28,44},{32,4... | collective-permute-start | bytes 18440
  628.9 78.1 %collective-permute-start.2 = (bf16[192,16]{0,1:T(8,128)(2,1)S(1)}, bf16[192,16]{0,1:T(8,128)(2,1)S(1)}, u32[]{:S(2)}, u32[]{:S(2)}) collective-permute-start(bf16[192,16]{0,1:T(8,128)(2,1)S(1)} %convert.108), channel_id=1, source_target_pairs={{0,12},{4,16},{8,20},{12,24},{16,28},{20,32},{24,36},{28,40},{32,4... | collective-permute-start | bytes 18440
  630.2 80.3 %collective-permute-start.1 = (bf16[192,16]{0,1:T(8,128)(2,1)S(1)}, bf16[192,16]{0,1:T(8,128)(2,1)S(1)}, u32[]{:S(2)}, u32[]{:S(2)}) collective-permute-start(bf16[192,16]{0,1:T(8,128)(2,1)S(1)} %convert.108), channel_id=1, source_target_pairs={{0,8},{4,12},{8,16},{12,20},{16,24},{20,28},{24,32},{28,36},{32,40... | collective-permute-start | bytes 18440
  631.5 90.3 %collective-permute-start = (bf16[192,16]{0,1:T(8,128)(2,1)S(1)}, bf16[192,16]{0,1:T(8,128)(2,1)S(1)}, u32[]{:S(2)}, u32[]{:S(2)}) collective-permute-start(bf16[192,16]{0,1:T(8,128)(2,1)S(1)} %convert.108), channel_id=1, source_target_pairs={{0,4},{4,8},{8,12},{12,16},{16,20},{20,24},{24,28},{28,32},{32,36}... | collective-permute-start | bytes 18440
  632.8 91.5 %collective-permute-start.30 = (bf16[16,192]{1,0:T(8,128)(2,1)S(1)}, bf16[16,192]{1,0:T(8,128)(2,1)S(1)}, u32[]{:S(2)}, u32[]{:S(2)}) collective-permute-start(bf16[16,192]{1,0:T(8,128)(2,1)S(1)} %convert.107), channel_id=1, source_target_pairs={{0,60},{4,64},{8,68},{12,72},{16,76},{20,80},{24,84},{28,88},{32,9... | collective-permute-start | bytes 18440
  697.4 28.9 %collective-permute-start.29 = (bf16[16,192]{1,0:T(8,128)(2,1)S(1)}, bf16[16,192]{1,0:T(8,128)(2,1)S(1)}, u32[]{:S(2)}, u32[]{:S(2)}) collective-permute-start(bf16[16,192]{1,0:T(8,128)(2,1)S(1)} %convert.107), channel_id=1, source_target_pairs={{0,56},{4,60},{8,64},{12,68},{16,72},{20,76},{24,80},{28,84},{32,8... | collective-permute-start | bytes 18440
  707.0 21.9 %collective-permute-start.28 = (bf16[16,192]{1,0:T(8,128)(2,1)S(1)}, bf16[16,192]{1,0:T(8,128)(2,1)S(1)}, u32[]{:S(2)}, u32[]{:S(2)}) collective-permute-start(bf16[16,192]{1,0:T(8,128)(2,1)S(1)} %convert.107), channel_id=1, source_target_pairs={{0,52},{4,56},{8,60},{12,64},{16,68},{20,72},{24,76},{28,80},{32,8... | collective-permute-start | bytes 18440
  710.5 21.5 %collective-permute-start.27 = (bf16[16,192]{1,0:T(8,128)(2,1)S(1)}, bf16[16,192]{1,0:T(8,128)(2,1)S(1)}, u32[]{:S(2)}, u32[]{:S(2)}) collective-permute-start(bf16[16,192]{1,0:T(8,128)(2,1)S(1)} %convert.107), channel_id=1, source_target_pairs={{0,48},{4,52},{8,56},{12,60},{16,64},{20,68},{24,72},{28,76},{32,8... | collective-permute-start | bytes 18440
  721.8 14.2 %collective-permute-start.26 = (bf16[16,192]{1,0:T(8,128)(2,1)S(1)}, bf16[16,192]{1,0:T(8,128)(2,1)S(1)}, u32[]{:S(2)}, u32[]{:S(2)}) collective-permute-start(bf16[16,192]{1,0:T(8,128)(2,1)S(1)} %convert.107), channel_id=1, source_target_pairs={{0,44},{4,48},{8,52},{12,56},{16,60},{20,64},{24,68},{28,72},{32,7... | collective-permute-start | bytes 18440
  724.3 13.9 %collective-permute-start.25 = (bf16[16,192]{1,0:T(8,128)(2,1)S(1)}, bf16[16,192]{1,0:T(8,128)(2,1)S(1)}, u32[]{:S(2)}, u32[]{:S(2)}) collective-permute-start(bf16[16,192]{1,0:T(8,128)(2,1)S(1)} %convert.107), channel_id=1, source_target_pairs={{0,40},{4,44},{8,48},{12,52},{16,56},{20,60},{24,64},{28,68},{32,7... | collective-permute-start | bytes 18440
  726.3 14.8 %collective-permute-start.24 = (bf16[16,192]{1,0:T(8,128)(2,1)S(1)}, bf16[16,192]{1,0:T(8,128)(2,1)S(1)}, u32[]{:S(2)}, u32[]{:S(2)}) collective-permute-start(bf16[16,192]{1,0:T(8,128)(2,1)S(1)} %convert.107), channel_id=1, source_target_pairs={{0,36},{4,40},{8,44},{12,48},{16,52},{20,56},{24,60},{28,64},{32,6... | collective-permute-start | bytes 18440
  728.9 15.6 %collective-permute-start.23 = (bf16[16,192]{1,0:T(8,128)(2,1)S(1)}, bf16[16,192]{1,0:T(8,128)(2,1)S(1)}, u32[]{:S(2)}, u32[]{:S(2)}) collective-permute-start(bf16[16,192]{1,0:T(8,128)(2,1)S(1)} %convert.107), channel_id=1, source_target_pairs={{0,32},{4,36},{8,40},{12,44},{16,48},{20,52},{24,56},{28,60},{32,6... | collective-permute-start | bytes 18440
  732.0 14.7 %collective-permute-start.22 = (bf16[16,192]{1,0:T(8,128)(2,1)S(1)}, bf16[16,192]{1,0:T(8,128)(2,1)S(1)}, u32[]{:S(2)}, u32[]{:S(2)}) collective-permute-start(bf16[16,192]{1,0:T(8,128)(2,1)S(1)} %convert.107), channel_id=1, source_target_pairs={{0,28},{4,32},{8,36},{12,40},{16,44},{20,48},{24,52},{28,56},{32,6... | collective-permute-start | bytes 18440
  736.0 13.2 %collective-permute-start.21 = (bf16[16,192]{1,0:T(8,128)(2,1)S(1)}, bf16[16,192]{1,0:T(8,128)(2,1)S(1)}, u32[]{:S(2)}, u32[]{:S(2)}) collective-permute-start(bf16[16,192]{1,0:T(8,128)(2,1)S(1)} %convert.107), channel_id=1, source_target_pairs={{0,24},{4,28},{8,32},{12,36},{16,40},{20,44},{24,48},{28,52},{32,5... | collective-permute-start | bytes 18440
  738.2 15.3 %collective-permute-start.20 = (bf16[16,192]{1,0:T(8,128)(2,1)S(1)}, bf16[16,192]{1,0:T(8,128)(2,1)S(1)}, u32[]{:S(2)}, u32[]{:S(2)}) collective-permute-start(bf16[16,192]{1,0:T(8,128)(2,1)S(1)} %convert.107), channel_id=1, source_target_pairs={{0,20},{4,24},{8,28},{12,32},{16,36},{20,40},{24,44},{28,48},{32,5... | collective-permute-start | bytes 18440
  741.1 13.8 %collective-permute-start.19 = (bf16[16,192]{1,0:T(8,128)(2,1)S(1)}, bf16[16,192]{1,0:T(8,128)(2,1)S(1)}, u32[]{:S(2)}, u32[]{:S(2)}) collective-permute-start(bf16[16,192]{1,0:T(8,128)(2,1)S(1)} %convert.107), channel_id=1, source_target_pairs={{0,16},{4,20},{8,24},{12,28},{16,32},{20,36},{24,40},{28,44},{32,4... | collective-permute-start | bytes 18440
  744.5 12.4 %collective-permute-start.18 = (bf16[16,192]{1,0:T(8,128)(2,1)S(1)}, bf16[16,192]{1,0:T(8,128)(2,1)S(1)}, u32[]{:S(2)}, u32[]{:S(2)}) collective-permute-start(bf16[16,192]{1,0:T(8,128)(2,1)S(1)} %convert.107), channel_id=1, source_target_pairs={{0,12},{4,16},{8,20},{12,24},{16,28},{20,32},{24,36},{28,40},{32,4... | collective-permute-start | bytes 18440
  746.7 11.5 %collective-permute-start.17 = (bf16[16,192]{1,0:T(8,128)(2,1)S(1)}, bf16[16,192]{1,0:T(8,128)(2,1)S(1)}, u32[]{:S(2)}, u32[]{:S(2)}) collective-permute-start(bf16[16,192]{1,0:T(8,128)(2,1)S(1)} %convert.107), channel_id=1, source_target_pairs={{0,8},{4,12},{8,16},{12,20},{16,24},{20,28},{24,32},{28,36},{32,40... | collective-permute-start | bytes 18440
  749.3 11.4 %collective-permute-start.16 = (bf16[16,192]{1,0:T(8,128)(2,1)S(1)}, bf16[16,192]{1,0:T(8,128)(2,1)S(1)}, u32[]{:S(2)}, u32[]{:S(2)}) collective-permute-start(bf16[16,192]{1,0:T(8,128)(2,1)S(1)} %convert.107), channel_id=1, source_target_pairs={{0,4},{4,8},{8,12},{12,16},{16,20},{20,24},{24,28},{28,32},{32,36}... | collective-permute-start | bytes 18440
  753.6 9.2 %collective-permute-start.47 = (bf16[768,6]{0,1:T(8,128)(2,1)S(1)}, bf16[768,6]{0,1:T(8,128)(2,1)S(1)}, u32[]{:S(2)}, u32[]{:S(2)}) collective-permute-start(bf16[768,6]{0,1:T(8,128)(2,1)S(1)} %slice.2), channel_id=1, source_target_pairs={{0,64},{4,68},{8,72},{12,76},{16,80},{20,84},{24,88},{28,92},{32,9... | collective-permute-start | bytes 27656
  754.9 12.4 %collective-permute-start.46 = (bf16[768,8]{0,1:T(8,128)(2,1)S(1)}, bf16[768,8]{0,1:T(8,128)(2,1)S(1)}, u32[]{:S(2)}, u32[]{:S(2)}) collective-permute-start(bf16[768,8]{0,1:T(8,128)(2,1)S(1)} %convert.106), channel_id=1, source_target_pairs={{0,60},{4,64},{8,68},{12,72},{16,76},{20,80},{24,84},{28,88},{32,9... | collective-permute-start | bytes 36872
  756.9 12.0 %collective-permute-start.45 = (bf16[768,8]{0,1:T(8,128)(2,1)S(1)}, bf16[768,8]{0,1:T(8,128)(2,1)S(1)}, u32[]{:S(2)}, u32[]{:S(2)}) collective-permute-start(bf16[768,8]{0,1:T(8,128)(2,1)S(1)} %convert.106), channel_id=1, source_target_pairs={{0,56},{4,60},{8,64},{12,68},{16,72},{20,76},{24,80},{28,84},{32,8... | collective-permute-start | bytes 36872
  758.3 14.1 %collective-permute-start.44 = (bf16[768,8]{0,1:T(8,128)(2,1)S(1)}, bf16[768,8]{0,1:T(8,128)(2,1)S(1)}, u32[]{:S(2)}, u32[]{:S(2)}) collective-permute-start(bf16[768,8]{0,1:T(8,128)(2,1)S(1)} %convert.106), channel_id=1, source_target_pairs={{0,52},{4,56},{8,60},{12,64},{16,68},{20,72},{24,76},{28,80},{32,8... | collective-permute-start | bytes 36872
  760.7 12.9 %collective-permute-start.43 = (bf16[768,8]{0,1:T(8,128)(2,1)S(1)}, bf16[768,8]{0,1:T(8,128)(2,1)S(1)}, u32[]{:S(2)}, u32[]{:S(2)}) collective-permute-start(bf16[768,8]{0,1:T(8,128)(2,1)S(1)} %convert.106), channel_id=1, source_target_pairs={{0,48},{4,52},{8,56},{12,60},{16,64},{20,68},{24,72},{28,76},{32,8... | collective-permute-start | bytes 36872
  762.8 15.2 %collective-permute-start.42 = (bf16[768,8]{0,1:T(8,128)(2,1)S(1)}, bf16[768,8]{0,1:T(8,128)(2,1)S(1)}, u32[]{:S(2)}, u32[]{:S(2)}) collective-permute-start(bf16[768,8]{0,1:T(8,128)(2,1)S(1)} %convert.106), channel_id=1, source_target_pairs={{0,44},{4,48},{8,52},{12,56},{16,60},{20,64},{24,68},{28,72},{32,7... | collective-permute-start | bytes 36872
  767.3 14.0 %collective-permute-start.41 = (bf16[768,8]{0,1:T(8,128)(2,1)S(1)}, bf16[768,8]{0,1:T(8,128)(2,1)S(1)}, u32[]{:S(2)}, u32[]{:S(2)}) collective-permute-start(bf16[768,8]{0,1:T(8,128)(2,1)S(1)} %convert.106), channel_id=1, source_target_pairs={{0,40},{4,44},{8,48},{12,52},{16,56},{20,60},{24,64},{28,68},{32,7... | collective-permute-start | bytes 36872
  769.0 14.9 %collective-permute-start.40 = (bf16[768,8]{0,1:T(8,128)(2,1)S(1)}, bf16[768,8]{0,1:T(8,128)(2,1)S(1)}, u32[]{:S(2)}, u32[]{:S(2)}) collective-permute-start(bf16[768,8]{0,1:T(8,128)(2,1)S(1)} %convert.106), channel_id=1, source_target_pairs={{0,36},{4,40},{8,44},{12,48},{16,52},{20,56},{24,60},{28,64},{32,6... | collective-permute-start | bytes 36872
  772.4 14.7 %collective-permute-start.39 = (bf16[768,8]{0,1:T(8,128)(2,1)S(1)}, bf16[768,8]{0,1:T(8,128)(2,1)S(1)}, u32[]{:S(2)}, u32[]{:S(2)}) collective-permute-start(bf16[768,8]{0,1:T(8,128)(2,1)S(1)} %convert.106), channel_id=1, source_target_pairs={{0,32},{4,36},{8,40},{12,44},{16,48},{20,52},{24,56},{28,60},{32,6... | collective-permute-start | bytes 36872
  773.7 15.9 %collective-permute-start.38 = (bf16[768,8]{0,1:T(8,128)(2,1)S(1)}, bf16[768,8]{0,1:T(8,128)(2,1)S(1)}, u32[]{:S(2)}, u32[]{:S(2)}) collective-permute-start(bf16[768,8]{0,1:T(8,128)(2,1)S(1)} %convert.106), channel_id=1, source_target_pairs={{0,28},{4,32},{8,36},{12,40},{16,44},{20,48},{24,52},{28,56},{32,6... | collective-permute-start | bytes 36872
  778.0 14.4 %collective-permute-start.37 = (bf16[768,8]{0,1:T(8,128)(2,1)S(1)}, bf16[768,8]{0,1:T(8,128)(2,1)S(1)}, u32[]{:S(2)}, u32[]{:S(2)}) collective-permute-start(bf16[768,8]{0,1:T(8,128)(2,1)S(1)} %convert.106), channel_id=1, source_target_pairs={{0,24},{4,28},{8,32},{12,36},{16,40},{20,44},{24,48},{28,52},{32,5... | collective-permute-start | bytes 36872
  781.3 14.9 %collective-permute-start.36 = (bf16[768,8]{0,1:T(8,128)(2,1)S(1)}, bf16[768,8]{0,1:T(8,128)(2,1)S(1)}, u32[]{:S(2)}, u32[]{:S(2)}) collective-permute-start(bf16[768,8]{0,1:T(8,128)(2,1)S(1)} %convert.106), channel_id=1, source_target_pairs={{0,20},{4,24},{8,28},{12,32},{16,36},{20,40},{24,44},{28,48},{32,5... | collective-permute-start | bytes 36872
  783.9 12.3 %collective-permute-start.35 = (bf16[768,8]{0,1:T(8,128)(2,1)S(1)}, bf16[768,8]{0,1:T(8,128)(2,1)S(1)}, u32[]{:S(2)}, u32[]{:S(2)}) collective-permute-start(bf16[768,8]{0,1:T(8,128)(2,1)S(1)} %convert.106), channel_id=1, source_target_pairs={{0,16},{4,20},{8,24},{12,28},{16,32},{20,36},{24,40},{28,44},{32,4... | collective-permute-start | bytes 36872
  787.1 9.1 %collective-permute-start.34 = (bf16[768,8]{0,1:T(8,128)(2,1)S(1)}, bf16[768,8]{0,1:T(8,128)(2,1)S(1)}, u32[]{:S(2)}, u32[]{:S(2)}) collective-permute-start(bf16[768,8]{0,1:T(8,128)(2,1)S(1)} %convert.106), channel_id=1, source_target_pairs={{0,12},{4,16},{8,20},{12,24},{16,28},{20,32},{24,36},{28,40},{32,4... | collective-permute-start | bytes 36872
  789.6 6.6 collective-permute-start.33
  (35 other events, 1126.9 us)
where the time goes:
time: 823 us; the launch traced here: 820 us
  blocking collectives  601 us (73%)
  starting transfers between devices  144 us (17%)
  matrix products  25.1 us (3%)
  local copies, waits for them, and re-layouts  18.1 us (2%)
  other arithmetic  17.8 us (2%)
  between operations  13.3 us (2%)
    psum x1, blocking collectives, on_device(): summed_delta = lax.psum(delta_part, 'dp')  301 us
    unnamed x2, blocking collectives  216 us
    unnamed x48, starting transfers between devices  137 us
    psum x1, blocking collectives, on_device(): squares = lax.psum(jnp.sum(summed_delta * summed_delta), 'strip')  61.9 us
    psum x1, blocking collectives, on_device(): lax.psum(shares[0].astype(jnp.bfloat16), 'strip').astype(jnp.float32)  16.7 us
  transfers between devices with their start and end apart: 49, of which 1 were waited for; matrix products, arithmetic and copies ran while one was open for 4% of the time, Pallas kernels for 0%

commit v1 on v0

v1 whole, which is shorter than its diff:
```python
import jax
import jax.numpy as jnp
import numpy as np
from jax import lax
from jax.experimental import pallas as pl
from jax.experimental.pallas import tpu as pltpu
from jax.sharding import PartitionSpec as P

KS = 7
EPS_NORM = 1e-06
EPS_ROOT = 1e-12
BOUND = 0.5
STEP_UNIT = 0.1

NZ, NY, NXH, NXL, NC = 8, 4, 2, 2, 2
NX = NXH * NXL
ROWS, COLS, CELLS = 8, 32, 256
C1, F1, C2, CLASSES = 192, 768, 384, 62
WIDE = 256
PIECE = 48

F32 = jnp.float32
BF16 = jnp.bfloat16
MESH = pl.DeviceIdType.MESH


def index_table():
    table = np.full((8, F1), -1, np.int32)

    def owner(x_hi, y, z):
        return (z * NY + y) * NXH + x_hi

    for x_hi in range(NXH):
        for y in range(NY):
            for z in range(NZ):
                own = owner(x_hi, y, z)
                for q in range(6):
                    place = ((x_hi * NY + y) * NZ + z) * 6 + q
                    table[0, place] = own * 12 + q
                    table[0, 384 + place] = own * 12 + 6 + q
                    table[1, place] = own * 6 + q
                    if q < 3:
                        table[2, place] = own * 3 + q
                    else:
                        table[3, place] = own * 3 + q - 3
    for part_col in range(4):
        for strip in range(4):
            for channel in range(3):
                for row in range(8):
                    lane = part_col * 128 + strip * 24 + channel * 8 + row
                    table[4, lane] = channel * 16 + (row % 4) * 4 + part_col
                    table[5, lane] = strip * 2 + row // 4
    return table


def dot_nn(a, b):
    return lax.dot_general(a, b, (((1,), (0,)), ((), ())), preferred_element_type=F32)


def dot_nt(a, b):
    return lax.dot_general(a, b, (((1,), (1,)), ((), ())), preferred_element_type=F32)


def dot_tn(a, b):
    return lax.dot_general(a, b, (((0,), (0,)), ((), ())), preferred_element_type=F32)


def mean_lanes(values):
    return jnp.sum(values, axis=-1, keepdims=True) * (1.0 / values.shape[-1])


def norm_parts(values):
    centred = values - mean_lanes(values)
    root = lax.rsqrt(mean_lanes(centred * centred) + EPS_NORM)
    return centred * root, root


def norm_back(unit, root, grad):
    return root * (grad - mean_lanes(grad) - unit * mean_lanes(grad * unit))


def one_hot(index_row, rows):
    width = index_row.shape[1]
    return (lax.broadcasted_iota(jnp.int32, (rows, width), 0) == index_row).astype(F32).astype(BF16)


def first_row(values, rows=16):
    wide = jnp.broadcast_to(values[0:1], (rows, values.shape[1])).astype(F32)
    return jnp.where(lax.broadcasted_iota(jnp.int32, wide.shape, 0) == 0, wide, 0.0).astype(BF16)


def image_kernel(
    label,
    pixels,
    delta,
    table,
    stem_weight,
    stem_gain,
    taps,
    norm1_gain,
    up_weight,
    down_weight,
    scale1,
    down_gain,
    ds_weight,
    head_gain,
    head_weight,
    loss_out,
    first_out,
    second_out,
    delta_out,
    padded,
    shifted,
    mixed_ref,
    wide_ref,
    tap_grad,
    taps_ref,
):
    taps_ref[...] = taps[...].astype(F32)
    perturbed = (pixels[...].astype(F32) + delta[...]).reshape(96, 128)
    perturbed = jnp.concatenate([perturbed, jnp.zeros((32, 128), F32)], axis=0).astype(BF16)
    i0 = lax.broadcasted_iota(jnp.int32, (128, 128), 0)
    i1 = lax.broadcasted_iota(jnp.int32, (128, 128), 1)
    column_pick = (i1 == 4 * (i0 & 31) + (i0 >> 5)).astype(F32).astype(BF16)
    columns = dot_nt(column_pick, perturbed)
    columns = jnp.concatenate([columns[32 * k : 32 * k + 32] for k in range(4)], axis=1)
    row_of = table[5:6, 0:512]
    cells = jnp.concatenate(
        [jnp.where(row_of == r, columns, 0.0) for r in range(ROWS)], axis=0
    ).astype(BF16)
    feature_pick = one_hot(table[4:5, 0:512], 48)
    patches = dot_nt(cells, feature_pick).astype(BF16)

    stem_pre = dot_nn(patches, stem_weight[...])
    stem_unit, stem_root = norm_parts(stem_pre)
    stem_out = (stem_unit * stem_gain[...]).astype(BF16).astype(F32)

    def spread_columns(values):
        padded[:, 8 : 8 + COLS, :] = values.reshape(ROWS, COLS, C1)
        for j in range(KS):
            shifted[j] = padded[:, 5 + j : 5 + j + COLS, :]

    padded[:, 0:8, :] = jnp.zeros((ROWS, 8, C1), F32)
    padded[:, 8 + COLS :, :] = jnp.zeros((ROWS, 8, C1), F32)
    spread_columns(stem_out)
    for r in range(ROWS):
        total = None
        for i in range(KS):
            if 0 <= r + i - 3 < ROWS:
                for j in range(KS):
                    tap = KS * i + j
                    term = shifted[j, r + i - 3] * taps_ref[tap : tap + 1, :]
                    total = term if total is None else total + term
        mixed_ref[r] = total
    mixed = mixed_ref[...].reshape(CELLS, C1)

    mixed_unit, mixed_root = norm_parts(mixed)
    normed = (mixed_unit * norm1_gain[...]).astype(BF16)
    upper = dot_nn(normed, up_weight[...])
    half = 0.5 + 0.5 * lax.erf(upper * (0.5**0.5))
    hidden = (upper * half).astype(BF16)
    gelu_slope = half + upper * jnp.exp(-0.5 * upper * upper) * ((2.0 * np.pi) ** -0.5)
    branch = dot_nn(hidden, down_weight[...])
    section = (stem_out + scale1[...] * branch).astype(BF16).astype(F32)

    section_unit, section_root = norm_parts(section)
    merged = (section_unit * down_gain[...]).astype(BF16)
    p0 = lax.broadcasted_iota(jnp.int32, (16, CELLS), 0)
    p1 = lax.broadcasted_iota(jnp.int32, (16, CELLS), 1)
    place_pick = (p0 == 2 * ((p1 >> 5) & 1) + (p1 & 1)).astype(F32).astype(BF16)
    merged_sum = dot_nn(place_pick, merged)
    sums_high = merged_sum.astype(BF16)
    rest = merged_sum - sums_high.astype(F32)
    sums_mid = rest.astype(BF16)
    sums_low = (rest - sums_mid.astype(F32)).astype(BF16)
    row16 = lax.broadcasted_iota(jnp.int32, (16, C1), 0)

    def place_rows(place):
        high = sums_high[place : place + 1].astype(F32)
        mid = sums_mid[place : place + 1].astype(F32)
        low = sums_low[place : place + 1].astype(F32)
        return jnp.where(
            row16 == 0, high, jnp.where(row16 == 1, mid, jnp.where(row16 == 2, low, 0.0))
        ).astype(BF16)

    split_sums = [place_rows(place) for place in range(4)]
    pooled = None
    for place in range(4):
        term = dot_nn(split_sums[place], ds_weight[place * C1 : (place + 1) * C1, :])
        pooled = term if pooled is None else pooled + term
    cells_two = CELLS // 4
    pooled = jnp.sum(pooled, axis=0, keepdims=True) * (1.0 / cells_two)
    pooled = jnp.broadcast_to(pooled, (16, C2))
    head_unit, head_root = norm_parts(pooled)
    head_in = (head_unit * head_gain[...]).astype(BF16)
    logits = dot_nn(head_in, head_weight[...])
    onehot = (lax.broadcasted_iota(jnp.int32, logits.shape, 1) == label[0]).astype(F32)
    top = jnp.max(logits, axis=-1, keepdims=True)
    raised = jnp.exp(logits - top)
    mass = jnp.sum(raised, axis=-1, keepdims=True)
    losses = jnp.log(mass) + top - jnp.sum(onehot * logits, axis=-1, keepdims=True)
    loss_out[0] = losses[0, 0]
    grad_logits = (raised / mass - onehot).astype(BF16)
    grad_head_in = dot_nt(grad_logits, head_weight[...])
    grad_pooled = norm_back(head_unit, head_root, grad_head_in * head_gain[...])
    grad_start = (grad_pooled * (1.0 / cells_two)).astype(BF16)

    unit_pick = one_hot(table[1:2, 0:C2], C2)
    start_rows = dot_nn(grad_start, unit_pick).astype(BF16)
    wide_rows = lax.broadcasted_iota(jnp.int32, (16, C2), 0)
    start_rows = jnp.where(wide_rows < 3, start_rows.astype(F32), 0.0).astype(BF16)
    for place in range(4):
        grad_ds = dot_tn(start_rows, split_sums[place]).astype(BF16)
        for x_hi in range(NXH):
            for y in range(NY):
                at = (x_hi * NY + y) * PIECE
                block = grad_ds[at : at + PIECE]
                if place % 2 == 0:
                    first_out[2 + place // 2, x_hi, y, :, 0:C1] = block
                else:
                    second_out[2 + place // 2, y, x_hi, :, 0:C1] = block
    o0 = lax.broadcasted_iota(jnp.int32, (64, WIDE), 0)
    o1 = lax.broadcasted_iota(jnp.int32, (64, WIDE), 1)
    offset_pick = (o1 == o0 + C1).astype(F32).astype(BF16)
    grad_logits_wide = jnp.concatenate([grad_logits.astype(F32), jnp.zeros((16, 2), F32)], axis=1)
    placed_logits = first_row(dot_nn(grad_logits_wide.astype(BF16), offset_pick))
    head_rows = dot_nn(head_in, unit_pick).astype(BF16)
    grad_head = dot_tn(head_rows, placed_logits)

    place_grads = [
        dot_nt(grad_start, ds_weight[place * C1 : (place + 1) * C1, :])[0:1] * down_gain[...]
        for place in range(4)
    ]
    even = (lax.broadcasted_iota(jnp.int32, (COLS, C1), 0) & 1) == 0
    by_row = [
        jnp.where(even, place_grads[2 * k], place_grads[2 * k + 1]) for k in range(2)
    ]
    grad_unit = jnp.concatenate([by_row[r % 2] for r in range(ROWS)], axis=0)
    grad_block = norm_back(section_unit, section_root, grad_unit).astype(BF16).astype(F32)

    grad_branch = (grad_block * scale1[...]).astype(BF16)
    grad_hidden = dot_nt(grad_branch, down_weight[...])
    grad_upper = (grad_hidden * gelu_slope).astype(BF16)
    grad_normed = dot_nt(grad_upper, up_weight[...])
    grad_mixed = norm_back(mixed_unit, mixed_root, grad_normed * norm1_gain[...])

    hidden_pick = one_hot(table[0:1, :], F1)

    def store_rows(strip, grads, extra):
        for x_hi in range(NXH):
            for y in range(NY):
                at = (x_hi * NY + y) * PIECE
                block = grads[at : at + PIECE]
                if extra is not None:
                    block = block + extra[at : at + PIECE]
                first_out[strip, x_hi, y] = block.astype(BF16)
                second_out[strip, y, x_hi] = grads[384 + at : 384 + at + PIECE].astype(BF16)

    wide_ref[...] = jnp.zeros((CELLS, WIDE), BF16)
    wide_ref[:, 0:C1] = normed
    grad_up = dot_tn(dot_nn(grad_upper, hidden_pick).astype(BF16), wide_ref[...])
    store_rows(0, grad_up, grad_head)

    mixed_ref[...] = grad_mixed.reshape(ROWS, COLS, C1)
    tap_grad[...] = jnp.zeros_like(tap_grad)
    for i in range(KS):
        for j in range(KS):
            total = None
            for r in range(ROWS):
                if 0 <= r + i - 3 < ROWS:
                    term = shifted[j, r + i - 3] * mixed_ref[r]
                    total = term if total is None else total + term
            tap = KS * i + j
            tap_grad[tap : tap + 1, :] = jnp.sum(total, axis=0, keepdims=True)

    spread_columns(grad_mixed)
    for r in range(ROWS):
        total = None
        for i in range(KS):
            if 0 <= r + i - 3 < ROWS:
                for j in range(KS):
                    tap = KS * (KS - 1 - i) + (KS - 1 - j)
                    term = shifted[j, r + i - 3] * taps_ref[tap : tap + 1, :]
                    total = term if total is None else total + term
        mixed_ref[r] = total
    grad_stem = grad_block + mixed_ref[...].reshape(CELLS, C1)
    grad_pre = norm_back(stem_unit, stem_root, grad_stem * stem_gain[...]).astype(BF16)

    grad_stem_weight = dot_tn(patches, grad_pre)
    stem_rows = dot_nn(grad_stem_weight.astype(BF16), one_hot(table[2:3, 0:C2], C1))
    tap_rows = dot_nn(tap_grad[...].astype(BF16), one_hot(table[3:4, 0:C2], C1))
    stem_rows = jnp.concatenate([stem_rows, jnp.zeros((16, C2), F32)], axis=0)
    grad_small = dot_tn((stem_rows + tap_rows).astype(BF16), offset_pick)
    wide_ref[:, 0:C1] = grad_branch
    grad_down = dot_tn(dot_nn(hidden, hidden_pick).astype(BF16), wide_ref[...])
    store_rows(1, grad_down, grad_small)

    grad_patches = dot_nt(grad_pre, stem_weight[...]).astype(BF16)
    grad_cells = dot_nn(grad_patches, feature_pick)
    grad_columns = None
    for r in range(ROWS):
        term = jnp.where(row_of == r, grad_cells[r * COLS : (r + 1) * COLS], 0.0)
        grad_columns = term if grad_columns is None else grad_columns + term
    grad_columns = grad_columns.astype(BF16)
    grad_pixels = None
    for k in range(4):
        term = dot_tn(
            grad_columns[:, 128 * k : 128 * k + 128], column_pick[32 * k : 32 * k + 32, :]
        )
        grad_pixels = term if grad_pixels is None else grad_pixels + term
    delta_out[...] = grad_pixels[0:96].reshape(4, 24, 128)


def places():
    dp, strip = lax.axis_index("dp"), lax.axis_index("strip")
    z, y, x_hi = dp // (NY * NXH), (dp // NXH) % NY, dp % NXH
    x_lo, core = strip // NC, strip % NC
    return dp, strip, z, y, x_hi, x_lo, core


def exchange_kernel(images, strip_delta, pixels, delta, send, recv, local):
    dp, strip = lax.axis_index("dp"), lax.axis_index("strip")
    barrier = pltpu.get_barrier_semaphore()
    for t in range(1, 4):
        pl.semaphore_signal(barrier, inc=1, device_id=(dp, (strip + t) % 4), device_id_type=MESH)
    own = [
        pltpu.make_async_copy(images.at[strip], pixels.at[strip], local.at[0]),
        pltpu.make_async_copy(strip_delta, delta.at[strip], local.at[1]),
    ]
    for copy in own:
        copy.start()
    pl.semaphore_wait(barrier, 3)
    copies = []
    for t in range(1, 4):
        peer = (strip + t) % 4
        for k, (source, target) in enumerate(
            ((images.at[peer], pixels.at[strip]), (strip_delta, delta.at[strip]))
        ):
            copies.append(
                pltpu.make_async_remote_copy(
                    src_ref=source,
                    dst_ref=target,
                    send_sem=send.at[t - 1, k],
                    recv_sem=recv.at[t - 1, k],
                    device_id=(dp, peer),
                    device_id_type=MESH,
                )
            )
    for copy in copies:
        copy.start()
    for copy in own + copies:
        copy.wait()


def reduce_kernel(
    first,
    second,
    delta,
    shares,
    delta_sum,
    squares,
    core_a,
    core_b,
    core_p,
    held_a,
    held_b,
    held_p,
    got_a,
    got_b,
    got_p,
    next_a,
    next_b,
    next_p,
    last_a,
    last_b,
    last_p,
    rows_a,
    rows_b,
    stage,
    low,
    got_z,
    low_p,
    send,
    recv,
):
    dp, strip, z, y, x_hi, x_lo, core = places()
    x = x_hi * NXL + x_lo

    def x_peer(t):
        other = (x + t) % NX
        other_hi, other_lo = other // NXL, other % NXL
        return other_hi, other_lo, ((z * NY + y) * NXH + other_hi, other_lo * NC + core)

    def y_peer(t):
        other = (y + t) % NY
        return other, ((z * NY + other) * NXH + x_hi, strip)

    def z_peer(t):
        other = (z + t) % NZ
        return other, ((other * NY + y) * NXH + x_hi, strip)

    def strip_peer(t):
        return (dp, (strip + t) % (NXL * NC))

    barrier = pltpu.get_barrier_semaphore()
    peers = [x_peer(t)[2] for t in range(1, NX)] + [y_peer(t)[1] for t in range(1, NY)]
    peers += [z_peer(t)[1] for t in range(1, NZ)] + [strip_peer(t) for t in range(1, 4)]
    for peer in peers:
        pl.semaphore_signal(barrier, inc=1, device_id=peer, device_id_type=MESH)
    pl.semaphore_wait(barrier, len(peers))

    count = [0]

    def ship(source, target, peer):
        k = count[0]
        count[0] += 1
        copy = pltpu.make_async_remote_copy(
            src_ref=source,
            dst_ref=target,
            send_sem=send.at[k],
            recv_sem=recv.at[k],
            device_id=peer,
            device_id_type=MESH,
        )
        copy.start()
        return copy

    def settle(copies):
        for copy in copies:
            copy.wait()

    partner = (dp, x_lo * NC + (1 - core))
    sent = []
    for lo in range(NXL):
        theirs = lo * NC + (1 - core)
        sent.append(ship(first.at[theirs], core_a.at[lo], partner))
        sent.append(ship(second.at[theirs], core_b.at[lo], partner))
        sent.append(ship(delta.at[theirs], core_p.at[lo], partner))
    settle(sent)
    for lo in range(NXL):
        mine = lo * NC + core
        held_a[lo] = (first[mine].astype(F32) + core_a[lo].astype(F32)).astype(BF16)
        for k in range(NY):
            held_b[k, lo] = (second[mine, k].astype(F32) + core_b[lo, k].astype(F32)).astype(BF16)
        held_p[lo] = delta[mine] + core_p[lo]

    sent = []
    for t in range(1, 4):
        other_hi, other_lo, peer = x_peer(t)
        sent.append(ship(held_a.at[other_lo, other_hi], got_a.at[t - 1], peer))
        sent.append(ship(held_p.at[other_lo], got_p.at[x], peer))
        other, peer = y_peer(t)
        sent.append(ship(held_b.at[other], got_b.at[t - 1], peer))
    got_p[x] = held_p[x_lo]
    settle(sent)
    total = held_a[x_lo, x_hi].astype(F32)
    for t in range(3):
        total = total + got_a[t].astype(F32)
    next_a[...] = total.astype(BF16)
    total = held_b[y].astype(F32)
    for t in range(3):
        total = total + got_b[t].astype(F32)
    next_b[...] = total.astype(BF16)
    next_p[...] = (got_p[0] + got_p[1]) + (got_p[2] + got_p[3])

    sent = []
    for t in range(1, 4):
        other, peer = y_peer(t)
        sent.append(ship(next_a.at[other], last_a.at[t - 1], peer))
        sent.append(ship(next_p, last_p.at[y], peer))
        other_hi, other_lo, peer = x_peer(t)
        sent.append(ship(next_b.at[other_lo, other_hi], last_b.at[t - 1], peer))
    last_p[y] = next_p[...]
    settle(sent)
    total = next_a[y].astype(F32)
    for t in range(3):
        total = total + last_a[t].astype(F32)
    rows_a[...] = total
    total = next_b[x_lo, x_hi].astype(F32)
    for t in range(3):
        total = total + last_b[t].astype(F32)
    rows_b[...] = total
    low_p[z] = ((last_p[0] + last_p[1]) + (last_p[2] + last_p[3])).astype(BF16)
    for k in range(NZ):
        stage[k, 12:16] = jnp.zeros((4, WIDE), F32)
        stage[k, 0:6] = rows_a[6 * k : 6 * k + 6]
        stage[k, 6:12] = rows_b[6 * k : 6 * k + 6]
    low[...] = stage[...].astype(BF16)

    sent = []
    for t in range(1, NZ):
        other, peer = z_peer(t)
        sent.append(ship(low.at[other], got_z.at[t - 1], peer))
        sent.append(ship(low_p.at[z], low_p.at[z], peer))
    settle(sent)
    total = stage[z]
    for t in range(NZ - 1):
        total = total + got_z[t].astype(F32)
    shares[strip] = total
    total = low_p[0].astype(F32)
    for k in range(1, NZ):
        total = total + low_p[k].astype(F32)
    delta_sum[...] = total
    square = total * total
    squares[strip] = square[0:8] + square[8:16] + square[16:24]

    sent = []
    for t in range(1, 4):
        peer = strip_peer(t)
        sent.append(ship(shares.at[strip], shares.at[strip], peer))
        sent.append(ship(squares.at[strip], squares.at[strip], peer))
    settle(sent)


N_COPIES = 6 + 9 + 9 + 14 + 6


def finish_kernel(
    levels,
    shares,
    delta_sum,
    squares,
    perturbation,
    new_out,
    stem_out,
    dw_out,
    up_out,
    down_out,
    ds_out,
    head_out,
):
    total = jnp.sum((squares[0] + squares[1]) + (squares[2] + squares[3]))
    spread = jnp.sqrt(jnp.full((8, 128), total, F32) * (1.0 / 12288) + EPS_ROOT)
    for channel in range(3):
        level = STEP_UNIT * levels[channel].astype(F32)
        step = level * delta_sum[8 * channel : 8 * channel + 8] / spread
        new_out[channel] = jnp.clip(perturbation[channel] + step, -BOUND, BOUND)
    up_out[...] = shares[0].T[0:C1, 0:12]
    down_out[...] = shares[1][0:12, 0:C1]
    for k in range(2):
        turned = shares[2 + k].T
        for half in range(2):
            place = 2 * k + half
            ds_out[place * C1 : (place + 1) * C1, :] = turned[0:C1, 6 * half : 6 * half + 6]
    head_out[...] = shares[0][0:6, C1 : C1 + CLASSES]
    turned = shares[1].T
    stem_out[...] = turned[C1 : C1 + 48, 0:3]
    dw_out[...] = turned[C1 : C1 + 49, 3:6]


VMEM = pl.BlockSpec(memory_space=pltpu.VMEM)
SMEM = pl.BlockSpec(memory_space=pltpu.SMEM)


def shaped(shape, dtype):
    return jax.ShapeDtypeStruct(shape, dtype)


def run_exchange(images, perturbation):
    return pl.pallas_call(
        exchange_kernel,
        name="strip_exchange",
        out_shape=(shaped((4, 3, 8, 128), BF16), shaped((4, 3, 8, 128), F32)),
        in_specs=[VMEM] * 2,
        out_specs=(VMEM, VMEM),
        scratch_shapes=[
            pltpu.SemaphoreType.DMA((3, 2)),
            pltpu.SemaphoreType.DMA((3, 2)),
            pltpu.SemaphoreType.DMA((2,)),
        ],
        compiler_params=pltpu.CompilerParams(collective_id=0, has_side_effects=True),
    )(images, perturbation)


def run_image(labels, *operands):
    return pl.pallas_call(
        image_kernel,
        name="image_step",
        out_shape=(
            shaped((1,), F32),
            shaped((4, NXH, NY, PIECE, WIDE), BF16),
            shaped((4, NY, NXH, PIECE, WIDE), BF16),
            shaped((4, 24, 128), F32),
        ),
        in_specs=[SMEM] + [VMEM] * len(operands),
        out_specs=(SMEM, VMEM, VMEM, VMEM),
        scratch_shapes=[
            pltpu.VMEM((ROWS, COLS + 16, C1), F32),
            pltpu.VMEM((KS, ROWS, COLS, C1), F32),
            pltpu.VMEM((ROWS, COLS, C1), F32),
            pltpu.VMEM((CELLS, WIDE), BF16),
            pltpu.VMEM((64, C1), F32),
            pltpu.VMEM((KS * KS, C1), F32),
        ],
        compiler_params=pltpu.CompilerParams(vmem_limit_bytes=48 * 1024 * 1024),
    )(labels, *operands)


def run_reduce(first, second, delta):
    half_a = (NXL, NXH, NY, PIECE, WIDE)
    return pl.pallas_call(
        reduce_kernel,
        name="grad_reduce",
        out_shape=(
            shaped((4, 16, WIDE), F32),
            shaped((24, 128), F32),
            shaped((4, 8, 128), F32),
        ),
        in_specs=[VMEM] * 3,
        out_specs=(VMEM,) * 3,
        scratch_shapes=[
            pltpu.VMEM(half_a, BF16),
            pltpu.VMEM((NXL, NY, NXH, PIECE, WIDE), BF16),
            pltpu.VMEM((NXL, 24, 128), F32),
            pltpu.VMEM(half_a, BF16),
            pltpu.VMEM((NY, NXL, NXH, PIECE, WIDE), BF16),
            pltpu.VMEM((NXL, 24, 128), F32),
            pltpu.VMEM((3, NY, PIECE, WIDE), BF16),
            pltpu.VMEM((3, NXL, NXH, PIECE, WIDE), BF16),
            pltpu.VMEM((NX, 24, 128), F32),
            pltpu.VMEM((NY, PIECE, WIDE), BF16),
            pltpu.VMEM((NXL, NXH, PIECE, WIDE), BF16),
            pltpu.VMEM((24, 128), F32),
            pltpu.VMEM((3, PIECE, WIDE), BF16),
            pltpu.VMEM((3, PIECE, WIDE), BF16),
            pltpu.VMEM((NY, 24, 128), F32),
            pltpu.VMEM((PIECE, WIDE), F32),
            pltpu.VMEM((PIECE, WIDE), F32),
            pltpu.VMEM((NZ, 16, WIDE), F32),
            pltpu.VMEM((NZ, 16, WIDE), BF16),
            pltpu.VMEM((NZ - 1, 16, WIDE), BF16),
            pltpu.VMEM((NZ, 24, 128), BF16),
            pltpu.SemaphoreType.DMA((N_COPIES,)),
            pltpu.SemaphoreType.DMA((N_COPIES,)),
        ],
        compiler_params=pltpu.CompilerParams(collective_id=1, has_side_effects=True),
    )(first, second, delta)


def run_finish(levels, shares, delta_sum, squares, perturbation):
    return pl.pallas_call(
        finish_kernel,
        name="finish",
        out_shape=(
            shaped((3, 8, 128), F32),
            shaped((48, 3), F32),
            shaped((49, 3), F32),
            shaped((C1, 12), F32),
            shaped((12, C1), F32),
            shaped((4 * C1, 6), F32),
            shaped((6, CLASSES), F32),
        ),
        in_specs=[SMEM] + [VMEM] * 4,
        out_specs=(VMEM,) * 7,
    )(levels, shares, delta_sum, squares, perturbation)


def on_device(
    images,
    perturbation,
    labels,
    step_levels,
    stem_weight,
    stem_gain,
    dw1_kernel,
    norm1_gain,
    up1_weight,
    down1_weight,
    scale1,
    down_gain,
    ds_weight,
    head_gain,
    head_weight,
):
    pixels, delta = run_exchange(images, perturbation)
    table = jnp.asarray(index_table())
    loss, first, second, delta_grad = run_image(
        labels,
        pixels,
        delta,
        table,
        stem_weight,
        stem_gain.reshape(1, C1),
        dw1_kernel,
        norm1_gain.reshape(1, C1),
        up1_weight,
        down1_weight,
        scale1.reshape(1, C1),
        down_gain.reshape(1, C1),
        ds_weight,
        head_gain.reshape(1, C2),
        head_weight,
    )
    shares, delta_sum, squares = run_reduce(first, second, delta_grad)
    new_delta, stem, dw, up, down, ds, head = run_finish(
        step_levels, shares, delta_sum, squares, perturbation
    )
    return (new_delta, loss, stem, dw, up, down, ds, head)


def solution(mesh):
    return jax.shard_map(
        on_device,
        mesh=mesh,
        in_specs=(
            P("dp", None, "strip", None),
            P(None, "strip", None),
            P(("dp", "strip")),
        )
        + (P(),) * 12,
        out_specs=(
            P(None, "strip", None),
            P(("dp", "strip")),
            P(None, "dp"),
            P(None, "dp"),
            P(None, "dp"),
            P("dp", None),
            P(None, "dp"),
            P("dp", None),
        ),
        check_vma=False,
    )
```

time: 823 us -> 67.3 us (0.08)
  blocking collectives: 601 us -> 0 us
  starting transfers between devices: 144 us -> 0 us
  Pallas kernels: 0 us -> 50.7 us
  matrix products: 25.1 us -> 0 us
  other arithmetic: 17.8 us -> 0 us
  between operations: 13.3 us -> 1.49 us
    psum x3 -> x0, blocking collectives: 379 us -> none  [the longest x1 301 us: on_device(): summed_delta = lax.psum(delta_part, 'dp')]
    unnamed x2 -> x0, blocking collectives: 216 us -> none
    unnamed x48 -> x0, starting transfers between devices: 137 us -> none
    pallas_call x0 -> x4, Pallas kernels: none -> 50.7 us  [the longest x1 31.2 us: run_reduce(): pl.pallas_call(reduce_kernel, name='grad_reduce', out_shape=(shaped((4, 1...]
    conv_general_dilated x3 -> x0, matrix products: 16.1 us -> none  [depthwise(): lax.conv_general_dilated(padded, taps, (1, 1), 'VALID', dimension_numbers...]
    dot_general x14 -> x0, matrix products: 8.98 us -> none  [the longest x5 4.35 us: dense(): result = jnp.dot(flattened, weight, preferred_element_type=jnp.float32)]
  transfers between devices with their start and end apart: 49 -> 0, of which waited for: 1 -> 0; matrix products, arithmetic and copies ran while one was open for 4% -> 0% of each run, Pallas kernels for 0% -> 0%
where the time goes in v1:
time: 67.3 us; the launch traced here: 66.6 us
  Pallas kernels  50.7 us (75%)
  local copies, waits for them, and re-layouts  14.4 us (21%)
  between operations  1.49 us (2%)
    pallas_call x1, Pallas kernels, run_reduce(): pl.pallas_call(reduce_kernel, name='grad_reduce', out_shape=(shaped((4, 1...  31.2 us
    unnamed x36, local copies, waits for them, and re-layouts  13.7 us
    pallas_call x1, Pallas kernels, run_image(): pl.pallas_call(image_kernel, name='image_step', out_shape=(shaped((1,), F...  9.47 us
    pallas_call x1, Pallas kernels, run_exchange(): pl.pallas_call(exchange_kernel, name='strip_exchange', out_shape=(shaped(...  8.12 us
    pallas_call x1, Pallas kernels, run_finish(): pl.pallas_call(finish_kernel, name='finish', out_shape=(shaped((3, 8, 128...  1.87 us

profile of v1, /device:TPU:1, one launch (start us, length us, event | category | flops | bytes accessed | tf_op | source)
XLA Modules:
  0.0 66.6 jit_solution(15718583694565053594)
XLA Ops:
  0.6 0.0 copy-start.2
  1.4 0.7 %reshape.35.head_gain = f32[1,384]{1,0:T(1,128)S(1)} reshape(f32[384]{0:T(512)} %param.29) | data formatting | bytes 3072 | tf_op jit(solution)/shard_map/reshape | solution.py:691
  2.0 8.1 %strip_exchange.1 = (bf16[4,3,8,128]{3,2,1,0:T(8,128)(2,1)}, f32[4,3,8,128]{3,2,1,0:T(8,128)}) custom-call(bf16[4,3,8,128]{3,2,1,0:T(8,128)(2,1)} %images.1, f32[3,8,128]{2,1,0:T(8,128)} %perturbation.1), custom_call_target="tpu_custom_call" | custom-call | tf_op jit(solution)/shard_map/strip_exchange/pallas_call | solution.py:560
  10.2 0.9 %copy.25.head_weight = bf16[384,62]{1,0:T(8,128)(2,1)S(1)} copy(bf16[384,62]{0,1:T(8,128)(2,1)} %param.30) | data formatting | bytes 95232 | tf_op args[14]
  11.1 0.0 copy-start.3
  11.1 0.0 copy-start.10
  11.1 0.0 copy-start.11
  11.1 0.0 copy-start.12
  11.1 0.0 copy-start.13
  11.2 1.2 %copy.24.down_weight = bf16[768,192]{1,0:T(8,128)(2,1)S(1)} copy(bf16[768,192]{0,1:T(8,128)(2,1)} %param.25) | data formatting | bytes 589824 | tf_op args[9]
  12.4 0.0 copy-done.2
  12.4 0.0 copy-done.3
  12.4 0.0 copy-done.10
  12.4 0.0 copy-done.11
  12.4 0.0 copy-done.12
  12.4 0.0 copy-done.13
  12.4 0.0 copy-start.5
  12.5 0.8 %copy-done.5 = f32[4,3,8,128]{3,2,1,0:T(8,128)S(1)} copy-done((f32[4,3,8,128]{3,2,1,0:T(8,128)S(1)}, f32[4,3,8,128]{3,2,1,0:T(8,128)}, u32[]{:S(2)}) %copy-start.5) | copy-done | bytes 49176
  13.2 0.0 copy-start.6
  13.2 0.7 %copy-done.6 = bf16[49,192]{1,0:T(8,128)(2,1)S(1)} copy-done((bf16[49,192]{1,0:T(8,128)(2,1)S(1)}, bf16[49,192]{1,0:T(8,128)(2,1)}, u32[]{:S(2)}) %copy-start.6) | copy-done | bytes 18840
  14.0 0.0 copy-start.7
  14.0 0.7 %copy-done.7 = bf16[48,192]{1,0:T(8,128)(2,1)S(1)} copy-done((bf16[48,192]{1,0:T(8,128)(2,1)S(1)}, bf16[48,192]{1,0:T(8,128)(2,1)}, u32[]{:S(2)}) %copy-start.7) | copy-done | bytes 18456
  14.7 0.0 copy-start.8
  14.7 0.7 %copy-done.8 = s32[8,768]{1,0:T(8,128)S(1)} copy-done((s32[8,768]{1,0:T(8,128)S(1)}, s32[8,768]{1,0:T(8,128)}, u32[]{:S(2)}) %copy-start.8) | copy-done | bytes 24600
  15.5 0.0 copy-start.9
  15.5 0.7 %copy-done.9 = bf16[4,3,8,128]{3,2,1,0:T(8,128)(2,1)S(1)} copy-done((bf16[4,3,8,128]{3,2,1,0:T(8,128)(2,1)S(1)}, bf16[4,3,8,128]{3,2,1,0:T(8,128)(2,1)}, u32[]{:S(2)}) %copy-start.9) | copy-done | bytes 24600
  16.2 9.5 %image_step.1 = (f32[1]{0:T(128)}, bf16[4,2,4,48,256]{4,3,2,1,0:T(8,128)(2,1)S(1)}, bf16[4,4,2,48,256]{4,3,2,1,0:T(8,128)(2,1)S(1)}, f32[4,24,128]{2,1,0:T(8,128)S(1)}) custom-call(s32[1]{0:T(128)S(6)} %copy.30.label, bf16[4,3,8,128]{3,2,1,0:T(8,128)(2,1)S(1)} %copy-done.9, f32[4,3,8,128]{3,2,1,0:T(8,128)S(1)} %copy-done.5, s32[8,768]{1,0:T(8,128)S(1)} %copy-done.8, ...), custom_call_target="tpu_custom_call" | custom-call | tf_op jit(solution)/shard_map/image_step/pallas_call | solution.py:576
  25.7 0.0 copy-start
  25.7 0.9 %copy-done = bf16[4,2,4,48,256]{4,3,2,1,0:T(8,128)(2,1)} copy-done((bf16[4,2,4,48,256]{4,3,2,1,0:T(8,128)(2,1)}, bf16[4,2,4,48,256]{4,3,2,1,0:T(8,128)(2,1)S(1)}, u32[]{:S(2)}) %copy-start) | copy-done | bytes 786456
  26.6 0.0 copy-start.1
  26.6 0.9 %copy-done.1 = bf16[4,4,2,48,256]{4,3,2,1,0:T(8,128)(2,1)} copy-done((bf16[4,4,2,48,256]{4,3,2,1,0:T(8,128)(2,1)}, bf16[4,4,2,48,256]{4,3,2,1,0:T(8,128)(2,1)S(1)}, u32[]{:S(2)}) %copy-start.1) | copy-done | bytes 786456
  27.5 0.0 copy-start.4
  27.5 0.6 copy-done.4
  28.1 31.2 %grad_reduce.1 = (f32[4,16,256]{2,1,0:T(8,128)}, f32[24,128]{1,0:T(8,128)}, f32[4,8,128]{2,1,0:T(8,128)}) custom-call(bf16[4,2,4,48,256]{4,3,2,1,0:T(8,128)(2,1)} %copy-done, bf16[4,4,2,48,256]{4,3,2,1,0:T(8,128)(2,1)} %copy-done.1, f32[4,24,128]{2,1,0:T(8,128)} %copy-done.4), custom_call_target="tpu_custom_call" | custom-call | tf_op jit(solution)/shard_map/grad_reduce/pallas_call | solution.py:601
  59.3 1.9 %finish.1 = (f32[3,8,128]{2,1,0:T(8,128)}, f32[48,3]{1,0:T(8,128)}, f32[49,3]{1,0:T(8,128)}, f32[192,12]{1,0:T(8,128)}, f32[12,192]{1,0:T(8,128)}, /*index=5*/f32[768,6]{1,0:T(8,128)}, f32[6,62]{1,0:T(8,128)}) custom-call(s32[3]{0:T(128)} %levels.1, f32[4,16,256]{2,1,0:T(8,128)} %get-tuple-element.29.shares, f32[24,128]{1,0:T(8,128)} %get-tuple-element.30.delta_sum, ...), custom_call_target="tpu_custom_call" | custom-call | tf_op jit(solution)/shard_map/finish/pallas_call | solution.py:641
  61.2 0.0 copy-start.14
  61.2 1.4 %copy.26 = f32[48,3]{0,1:T(4,128)} copy(f32[48,3]{1,0:T(8,128)} %get-tuple-element.42) | data formatting | bytes 1152
  62.6 0.0 copy-done.14
  62.6 0.7 copy.27
  63.2 1.6 %copy.28 = f32[192,12]{0,1:T(8,128)} copy(f32[192,12]{1,0:T(8,128)} %get-tuple-element.44) | data formatting | bytes 18432
  64.8 1.8 %copy.29 = f32[768,6]{0,1:T(8,128)} copy(f32[768,6]{1,0:T(8,128)} %get-tuple-element.46) | data formatting | bytes 36864
Async XLA Ops:
  0.6 11.8 %copy-start.2 = (bf16[768,384]{1,0:T(8,128)(2,1)S(1)}, bf16[768,384]{1,0:T(8,128)(2,1)}, u32[]{:S(2)}) copy-start(bf16[768,384]{1,0:T(8,128)(2,1)} %ds_weight.1) | copy-start | bytes 1769476
  11.1 1.3 %copy-start.3 = (bf16[192,768]{1,0:T(8,128)(2,1)S(1)}, bf16[192,768]{1,0:T(8,128)(2,1)}, u32[]{:S(2)}) copy-start(bf16[192,768]{1,0:T(8,128)(2,1)} %up_weight.1) | copy-start | bytes 884740
  11.1 1.3 %copy-start.10 = (f32[192]{0:T(256)S(1)}, f32[192]{0:T(256)}, u32[]{:S(2)}) copy-start(f32[192]{0:T(256)} %param.21) | copy-start | bytes 2308
  11.1 1.3 %copy-start.11 = (f32[192]{0:T(256)S(1)}, f32[192]{0:T(256)}, u32[]{:S(2)}) copy-start(f32[192]{0:T(256)} %param.23) | copy-start | bytes 2308
  11.1 1.3 %copy-start.12 = (f32[192]{0:T(256)S(1)}, f32[192]{0:T(256)}, u32[]{:S(2)}) copy-start(f32[192]{0:T(256)} %param.26) | copy-start | bytes 2308
  11.1 1.3 %copy-start.13 = (f32[192]{0:T(256)S(1)}, f32[192]{0:T(256)}, u32[]{:S(2)}) copy-start(f32[192]{0:T(256)} %param.27) | copy-start | bytes 2308
  12.4 0.8 %copy-start.5 = (f32[4,3,8,128]{3,2,1,0:T(8,128)S(1)}, f32[4,3,8,128]{3,2,1,0:T(8,128)}, u32[]{:S(2)}) copy-start(f32[4,3,8,128]{3,2,1,0:T(8,128)} %get-tuple-element.25.delta) | copy-start | bytes 147460
  13.2 0.7 %copy-start.6 = (bf16[49,192]{1,0:T(8,128)(2,1)S(1)}, bf16[49,192]{1,0:T(8,128)(2,1)}, u32[]{:S(2)}) copy-start(bf16[49,192]{1,0:T(8,128)(2,1)} %taps.1) | copy-start | bytes 56452
  14.0 0.7 %copy-start.7 = (bf16[48,192]{1,0:T(8,128)(2,1)S(1)}, bf16[48,192]{1,0:T(8,128)(2,1)}, u32[]{:S(2)}) copy-start(bf16[48,192]{1,0:T(8,128)(2,1)} %stem_weight.1) | copy-start | bytes 55300
  14.7 0.7 %copy-start.8 = (s32[8,768]{1,0:T(8,128)S(1)}, s32[8,768]{1,0:T(8,128)}, u32[]{:S(2)}) copy-start(s32[8,768]{1,0:T(8,128)} %constant.2.clone.table) | copy-start | bytes 73732
  15.5 0.7 %copy-start.9 = (bf16[4,3,8,128]{3,2,1,0:T(8,128)(2,1)S(1)}, bf16[4,3,8,128]{3,2,1,0:T(8,128)(2,1)}, u32[]{:S(2)}) copy-start(bf16[4,3,8,128]{3,2,1,0:T(8,128)(2,1)} %get-tuple-element.24.pixels) | copy-start | bytes 73732
  25.7 0.9 %copy-start = (bf16[4,2,4,48,256]{4,3,2,1,0:T(8,128)(2,1)}, bf16[4,2,4,48,256]{4,3,2,1,0:T(8,128)(2,1)S(1)}, u32[]{:S(2)}) copy-start(bf16[4,2,4,48,256]{4,3,2,1,0:T(8,128)(2,1)S(1)} %get-tuple-element.26.first) | copy-start | bytes 2359300
  26.6 0.9 %copy-start.1 = (bf16[4,4,2,48,256]{4,3,2,1,0:T(8,128)(2,1)}, bf16[4,4,2,48,256]{4,3,2,1,0:T(8,128)(2,1)S(1)}, u32[]{:S(2)}) copy-start(bf16[4,4,2,48,256]{4,3,2,1,0:T(8,128)(2,1)S(1)} %get-tuple-element.27.second) | copy-start | bytes 2359300
  27.5 0.6 copy-start.4
  61.2 1.4 %copy-start.14 = (f32[49,3]{1,0:T(8,128)S(1)}, f32[49,3]{1,0:T(8,128)}, u32[]{:S(2)}) copy-start(f32[49,3]{1,0:T(8,128)} %get-tuple-element.43) | copy-start | bytes 1768

commit v2 on v1

v2 whole, which is shorter than its diff:
```python
import jax
import jax.numpy as jnp
import numpy as np
from jax import lax
from jax.experimental import pallas as pl
from jax.experimental.pallas import tpu as pltpu
from jax.sharding import PartitionSpec as P

KS = 7
EPS_NORM = 1e-06
EPS_ROOT = 1e-12
BOUND = 0.5
STEP_UNIT = 0.1

NZ, NY, NXH, NXL, NC = 8, 4, 2, 2, 2
NX = NXH * NXL
ROWS, COLS, CELLS = 8, 32, 256
C1, F1, C2, CLASSES = 192, 768, 384, 62
WIDE = 256
PIECE = 48

F32 = jnp.float32
BF16 = jnp.bfloat16
MESH = pl.DeviceIdType.MESH


def index_table():
    table = np.full((8, F1), -1, np.int32)
    slots = {(0, 0): (2, 0), (0, 1): (6, 1), (1, 0): (2, 2), (1, 1): (7, 0), (2, 0): (3, 1), (2, 1): (7, 2)}
    for x_hi in range(NXH):
        for y in range(NY):
            for z in range(NZ):
                own = (z * NY + y) * NXH + x_hi
                block = (x_hi * NY + y) * NZ + z
                for q in range(6):
                    table[0, 6 * block + q] = own * 12 + q
                    table[0, 384 + 6 * block + q] = own * 12 + 6 + q
                    table[1, 6 * block + q] = own * 6 + q
                for (strip, _), (row, column) in slots.items():
                    table[row, strip * 64 + block] = own * 3 + column
    for part_col in range(4):
        for strip in range(4):
            for channel in range(3):
                for row in range(8):
                    lane = part_col * 128 + strip * 24 + channel * 8 + row
                    table[4, lane] = channel * 16 + (row % 4) * 4 + part_col
                    table[5, lane] = strip * 2 + row // 4
    return table


def dot_nn(a, b):
    return lax.dot_general(a, b, (((1,), (0,)), ((), ())), preferred_element_type=F32)


def dot_nt(a, b):
    return lax.dot_general(a, b, (((1,), (1,)), ((), ())), preferred_element_type=F32)


def dot_tn(a, b):
    return lax.dot_general(a, b, (((0,), (0,)), ((), ())), preferred_element_type=F32)


def mean_lanes(values):
    return jnp.sum(values, axis=-1, keepdims=True) * (1.0 / values.shape[-1])


def norm_parts(values):
    centred = values - mean_lanes(values)
    root = lax.rsqrt(mean_lanes(centred * centred) + EPS_NORM)
    return centred * root, root


def norm_back(unit, root, grad):
    return root * (grad - mean_lanes(grad) - unit * mean_lanes(grad * unit))


def one_hot(index_row, rows):
    width = index_row.shape[1]
    return (lax.broadcasted_iota(jnp.int32, (rows, width), 0) == index_row).astype(F32).astype(BF16)


def first_row(values, rows=16):
    wide = jnp.broadcast_to(values[0:1], (rows, values.shape[1])).astype(F32)
    return jnp.where(lax.broadcasted_iota(jnp.int32, wide.shape, 0) == 0, wide, 0.0).astype(BF16)


def step_kernel(
    label,
    head_gain,
    images,
    strip_delta,
    table_in,
    stem_in,
    stem_gain_in,
    taps_in,
    norm1_in,
    up_in,
    down_in,
    scale_in,
    down_gain_in,
    ds_in,
    head_in_t,
    shares,
    misc,
    pixels,
    delta,
    table,
    stem_weight,
    stem_gain,
    taps,
    norm1_gain,
    up_weight,
    down_weight,
    scale1,
    down_gain,
    ds_weight,
    head_weight,
    padded,
    shifted,
    mixed_ref,
    wide_merged,
    wide_normed,
    wide_branch,
    tap_grad,
    taps_ref,
    hidden_pick,
    unit_pick,
    ds_lo,
    ds_hi,
    ud_lo,
    ud_hi,
    small,
    delta_grad,
    c_ds_lo,
    c_ds_hi,
    c_ud_lo,
    c_ud_hi,
    c_small,
    c_delta,
    h_ds_lo,
    h_ds_hi,
    h_ud_lo,
    h_ud_hi,
    h_small,
    h_delta,
    x_ds_lo,
    x_ds_hi,
    x_ud_lo,
    x_ud_hi,
    x_small,
    x_delta,
    n_ds_lo,
    n_ds_hi,
    n_ud_lo,
    n_ud_hi,
    n_small,
    n_delta,
    y_ds_lo,
    y_ds_hi,
    y_ud_lo,
    y_ud_hi,
    y_small,
    y_delta,
    rows_ds,
    rows_ud,
    rows_small,
    stage,
    low,
    got_z,
    low_delta,
    local,
    send,
    recv,
):
    dp, strip = lax.axis_index("dp"), lax.axis_index("strip")
    z, y, x_hi = dp // (NY * NXH), (dp // NXH) % NY, dp % NXH
    x_lo, core = strip // NC, strip % NC
    x = x_hi * NXL + x_lo

    def x_peer(t):
        other = (x + t) % NX
        other_hi, other_lo = other // NXL, other % NXL
        return other_hi, other_lo, ((z * NY + y) * NXH + other_hi, other_lo * NC + core)

    def y_peer(t):
        other = (y + t) % NY
        return other, ((z * NY + other) * NXH + x_hi, strip)

    def z_peer(t):
        other = (z + t) % NZ
        return other, ((other * NY + y) * NXH + x_hi, strip)

    def strip_peer(t):
        return (strip + t) % (NXL * NC)

    barrier = pltpu.get_barrier_semaphore()
    peers = [(dp, strip_peer(t)) for t in range(1, 4)]
    peers += [x_peer(t)[2] for t in range(1, NX)] + [y_peer(t)[1] for t in range(1, NY)]
    peers += [z_peer(t)[1] for t in range(1, NZ)]
    for peer in peers:
        pl.semaphore_signal(barrier, inc=1, device_id=peer, device_id_type=MESH)

    loads = {}
    for k, (name, source, target) in enumerate(
        (
            ("table", table_in, table),
            ("pixels", images.at[strip], pixels.at[strip]),
            ("delta", strip_delta, delta.at[strip]),
            ("stem", stem_in, stem_weight),
            ("stem_gain", stem_gain_in, stem_gain),
            ("taps", taps_in, taps),
            ("norm1", norm1_in, norm1_gain),
            ("up", up_in, up_weight),
            ("down", down_in, down_weight),
            ("scale", scale_in, scale1),
            ("down_gain", down_gain_in, down_gain),
            ("ds", ds_in, ds_weight),
            ("head", head_in_t, head_weight),
        )
    ):
        loads[name] = pltpu.make_async_copy(source, target, local.at[k])
        loads[name].start()

    count = [0]

    def ship(source, target, peer):
        k = count[0]
        count[0] += 1
        copy = pltpu.make_async_remote_copy(
            src_ref=source,
            dst_ref=target,
            send_sem=send.at[k],
            recv_sem=recv.at[k],
            device_id=peer,
            device_id_type=MESH,
        )
        copy.start()
        return copy

    def settle(copies):
        for copy in copies:
            copy.wait()

    wide_merged[...] = jnp.zeros((CELLS, WIDE), BF16)
    wide_normed[...] = jnp.zeros((CELLS, WIDE), BF16)
    wide_branch[...] = jnp.zeros((CELLS, WIDE), BF16)
    tap_grad[...] = jnp.zeros_like(tap_grad)
    padded[:, 0:8, :] = jnp.zeros((ROWS, 8, C1), F32)
    padded[:, 8 + COLS :, :] = jnp.zeros((ROWS, 8, C1), F32)
    loads["table"].wait()
    hidden_pick[...] = one_hot(table[0:1, :], F1)
    unit_pick[...] = one_hot(table[1:2, 0:C2], C2)
    loads["taps"].wait()
    taps_ref[...] = taps[...].astype(F32)
    pl.semaphore_wait(barrier, len(peers))

    sent = []
    for t in range(1, 4):
        peer = strip_peer(t)
        sent.append(ship(images.at[peer], pixels.at[strip], (dp, peer)))
        sent.append(ship(strip_delta, delta.at[strip], (dp, peer)))
    for name in (
        "pixels", "delta", "stem", "stem_gain", "norm1", "up", "down", "scale", "down_gain", "ds", "head"
    ):
        loads[name].wait()
    settle(sent)

    perturbed = (pixels[...].astype(F32) + delta[...]).reshape(96, 128)
    perturbed = jnp.concatenate([perturbed, jnp.zeros((32, 128), F32)], axis=0).astype(BF16)
    i0 = lax.broadcasted_iota(jnp.int32, (128, 128), 0)
    i1 = lax.broadcasted_iota(jnp.int32, (128, 128), 1)
    column_pick = (i1 == 4 * (i0 & 31) + (i0 >> 5)).astype(F32).astype(BF16)
    columns = dot_nt(column_pick, perturbed)
    columns = jnp.concatenate([columns[32 * k : 32 * k + 32] for k in range(4)], axis=1)
    row_of = table[5:6, 0:512]
    cells = jnp.concatenate(
        [jnp.where(row_of == r, columns, 0.0) for r in range(ROWS)], axis=0
    ).astype(BF16)
    feature_pick = one_hot(table[4:5, 0:512], 48)
    patches = dot_nt(cells, feature_pick).astype(BF16)

    stem_pre = dot_nn(patches, stem_weight[...])
    stem_unit, stem_root = norm_parts(stem_pre)
    stem_out = (stem_unit * stem_gain[...]).astype(BF16).astype(F32)

    def spread_columns(values):
        padded[:, 8 : 8 + COLS, :] = values.reshape(ROWS, COLS, C1)
        for j in range(KS):
            shifted[j] = padded[:, 5 + j : 5 + j + COLS, :]

    def correlate(tap_of):
        for r in range(ROWS):
            total = None
            for i in range(KS):
                if 0 <= r + i - 3 < ROWS:
                    for j in range(KS):
                        tap = tap_of(i, j)
                        term = shifted[j, r + i - 3] * taps_ref[tap : tap + 1, :]
                        total = term if total is None else total + term
            mixed_ref[r] = total
        return mixed_ref[...].reshape(CELLS, C1)

    spread_columns(stem_out)
    mixed = correlate(lambda i, j: KS * i + j)

    mixed_unit, mixed_root = norm_parts(mixed)
    normed = (mixed_unit * norm1_gain[...]).astype(BF16)
    wide_normed[:, 0:C1] = normed
    upper = dot_nn(normed, up_weight[...])
    half = 0.5 + 0.5 * lax.erf(upper * (0.5**0.5))
    hidden = (upper * half).astype(BF16)
    gelu_slope = half + upper * jnp.exp(-0.5 * upper * upper) * ((2.0 * np.pi) ** -0.5)
    branch = dot_nt(hidden, down_weight[...])
    section = (stem_out + scale1[...] * branch).astype(BF16).astype(F32)

    section_unit, section_root = norm_parts(section)
    wide_merged[:, 0:C1] = (section_unit * down_gain[...]).astype(BF16)
    p0 = lax.broadcasted_iota(jnp.int32, (16, CELLS), 0)
    p1 = lax.broadcasted_iota(jnp.int32, (16, CELLS), 1)
    place_pick = (p0 == 2 * ((p1 >> 5) & 1) + (p1 & 1)).astype(F32).astype(BF16)
    merged_sum = dot_nn(place_pick, wide_merged[...])
    sums_high = merged_sum.astype(BF16).astype(F32)
    rest = merged_sum - sums_high
    sums_mid = rest.astype(BF16).astype(F32)
    sums_low = rest - sums_mid
    row16 = lax.broadcasted_iota(jnp.int32, (16, WIDE), 0)

    def place_rows(place):
        high = sums_high[place : place + 1]
        mid = sums_mid[place : place + 1]
        lowest = sums_low[place : place + 1]
        return jnp.where(
            row16 == 0, high, jnp.where(row16 == 1, mid, jnp.where(row16 == 2, lowest, 0.0))
        ).astype(BF16)

    split_sums = [place_rows(place) for place in range(4)]
    pooled = None
    for place in range(4):
        term = dot_nn(split_sums[place][:, 0:C1], ds_weight[place * C1 : (place + 1) * C1, :])
        pooled = term if pooled is None else pooled + term
    cells_two = CELLS // 4
    pooled = jnp.sum(pooled, axis=0, keepdims=True) * (1.0 / cells_two)
    pooled = jnp.broadcast_to(pooled, (16, C2))
    head_unit, head_root = norm_parts(pooled)
    gain = head_gain[...].reshape(1, C2)
    head_in = (head_unit * gain).astype(BF16)
    logits = dot_nt(head_in, head_weight[...])
    onehot = (lax.broadcasted_iota(jnp.int32, logits.shape, 1) == label[0]).astype(F32)
    top = jnp.max(logits, axis=-1, keepdims=True)
    raised = jnp.exp(logits - top)
    mass = jnp.sum(raised, axis=-1, keepdims=True)
    losses = jnp.log(mass) + top - jnp.sum(onehot * logits, axis=-1, keepdims=True)
    misc[3] = jnp.broadcast_to(losses[0:8], (8, 128))
    grad_logits = (raised / mass - onehot).astype(BF16)
    grad_head_in = dot_nn(grad_logits, head_weight[...])
    grad_pooled = norm_back(head_unit, head_root, grad_head_in * gain)
    grad_start = (grad_pooled * (1.0 / cells_two)).astype(BF16)

    def store_rows(first, second, at_strip, grads):
        for hi in range(NXH):
            for k in range(NY):
                at = (hi * NY + k) * PIECE
                block = grads[at : at + PIECE].astype(BF16)
                first[at_strip, hi, k] = block[:, 0:128]
                second[at_strip, k, hi] = block[:, 128:256]

    start_rows = dot_nn(grad_start, unit_pick[...])
    wide_rows = lax.broadcasted_iota(jnp.int32, (16, C2), 0)
    start_rows = jnp.where(wide_rows < 3, start_rows, 0.0).astype(BF16)
    o0 = lax.broadcasted_iota(jnp.int32, (64, WIDE), 0)
    o1 = lax.broadcasted_iota(jnp.int32, (64, WIDE), 1)
    head_offset = (o1 == o0 + C1).astype(F32).astype(BF16)
    grad_logits_wide = jnp.concatenate([grad_logits.astype(F32), jnp.zeros((16, 2), F32)], axis=1)
    placed_logits = first_row(dot_nn(grad_logits_wide.astype(BF16), head_offset))
    head_rows = dot_nn(head_in, unit_pick[...]).astype(BF16)
    for place in range(4):
        grad_ds = dot_tn(start_rows, split_sums[place])
        if place == 0:
            grad_ds = grad_ds + dot_tn(head_rows, placed_logits)
        store_rows(ds_lo, ds_hi, place, grad_ds)

    def core_start(*pairs):
        copies = []
        partner = (dp, x_lo * NC + (1 - core))
        for lo in range(NXL):
            for source, target in pairs:
                copies.append(ship(source.at[lo * NC + (1 - core)], target.at[lo], partner))
        return copies

    def core_sum(own_lo, own_hi, got_lo, got_hi, held_lo, held_hi):
        for lo in range(NXL):
            mine = lo * NC + core
            held_lo[lo] = (own_lo[mine].astype(F32) + got_lo[lo].astype(F32)).astype(BF16)
            for k in range(NY):
                block = own_hi[mine, k].astype(F32) + got_hi[lo, k].astype(F32)
                held_hi[k, lo] = block.astype(BF16)

    def first_start(held_lo, held_hi, got_lo, got_hi):
        copies = []
        for t in range(1, 4):
            other_hi, other_lo, peer = x_peer(t)
            copies.append(ship(held_lo.at[other_lo, other_hi], got_lo.at[t - 1], peer))
            other, peer = y_peer(t)
            copies.append(ship(held_hi.at[other], got_hi.at[t - 1], peer))
        return copies

    def first_sum(held_lo, held_hi, got_lo, got_hi, next_lo, next_hi):
        total = held_lo[x_lo, x_hi].astype(F32)
        for t in range(3):
            total = total + got_lo[t].astype(F32)
        next_lo[...] = total.astype(BF16)
        total = held_hi[y].astype(F32)
        for t in range(3):
            total = total + got_hi[t].astype(F32)
        next_hi[...] = total.astype(BF16)

    def second_start(next_lo, next_hi, got_lo, got_hi):
        copies = []
        for t in range(1, 4):
            other, peer = y_peer(t)
            copies.append(ship(next_lo.at[other], got_lo.at[t - 1], peer))
            other_hi, other_lo, peer = x_peer(t)
            copies.append(ship(next_hi.at[other_lo, other_hi], got_hi.at[t - 1], peer))
        return copies

    def second_sum(next_lo, next_hi, got_lo, got_hi, rows):
        total = next_lo[y].astype(F32)
        for t in range(3):
            total = total + got_lo[t].astype(F32)
        rows[:, 0:128] = total
        total = next_hi[x_lo, x_hi].astype(F32)
        for t in range(3):
            total = total + got_hi[t].astype(F32)
        rows[:, 128:256] = total

    core_ds = core_start((ds_lo, c_ds_lo), (ds_hi, c_ds_hi))

    place_grads = [
        dot_nt(grad_start, ds_weight[place * C1 : (place + 1) * C1, :])[0:1] * down_gain[...]
        for place in range(4)
    ]
    even = (lax.broadcasted_iota(jnp.int32, (COLS, C1), 0) & 1) == 0
    by_row = [
        jnp.where(even, place_grads[2 * k], place_grads[2 * k + 1]) for k in range(2)
    ]
    grad_unit = jnp.concatenate([by_row[r % 2] for r in range(ROWS)], axis=0)
    grad_block = norm_back(section_unit, section_root, grad_unit).astype(BF16).astype(F32)

    grad_branch = (grad_block * scale1[...]).astype(BF16)
    wide_branch[:, 0:C1] = grad_branch
    grad_down = dot_tn(dot_nn(hidden, hidden_pick[...]).astype(BF16), wide_branch[...])
    store_rows(ud_lo, ud_hi, 2, grad_down[0:384])
    store_rows(ud_lo, ud_hi, 3, grad_down[384:768])
    grad_hidden = dot_nn(grad_branch, down_weight[...])
    grad_upper = (grad_hidden * gelu_slope).astype(BF16)
    grad_up = dot_tn(dot_nn(grad_upper, hidden_pick[...]).astype(BF16), wide_normed[...])
    store_rows(ud_lo, ud_hi, 0, grad_up[0:384])
    store_rows(ud_lo, ud_hi, 1, grad_up[384:768])
    core_ud = core_start((ud_lo, c_ud_lo), (ud_hi, c_ud_hi))

    settle(core_ds)
    core_sum(ds_lo, ds_hi, c_ds_lo, c_ds_hi, h_ds_lo, h_ds_hi)
    first_ds = first_start(h_ds_lo, h_ds_hi, x_ds_lo, x_ds_hi)

    grad_normed = dot_nt(grad_upper, up_weight[...])
    grad_mixed = norm_back(mixed_unit, mixed_root, grad_normed * norm1_gain[...])

    mixed_ref[...] = grad_mixed.reshape(ROWS, COLS, C1)
    for i in range(KS):
        for j in range(KS):
            total = None
            for r in range(ROWS):
                if 0 <= r + i - 3 < ROWS:
                    term = shifted[j, r + i - 3] * mixed_ref[r]
                    total = term if total is None else total + term
            tap = KS * i + j
            tap_grad[tap : tap + 1, :] = jnp.sum(total, axis=0, keepdims=True)

    settle(core_ud)
    core_sum(ud_lo, ud_hi, c_ud_lo, c_ud_hi, h_ud_lo, h_ud_hi)
    first_ud = first_start(h_ud_lo, h_ud_hi, x_ud_lo, x_ud_hi)

    spread_columns(grad_mixed)
    grad_stem = grad_block + correlate(lambda i, j: KS * (KS - 1 - i) + (KS - 1 - j))
    grad_pre = norm_back(stem_unit, stem_root, grad_stem * stem_gain[...]).astype(BF16)

    grad_patches = dot_nt(grad_pre, stem_weight[...]).astype(BF16)
    grad_cells = dot_nn(grad_patches, feature_pick)
    grad_columns = None
    for r in range(ROWS):
        term = jnp.where(row_of == r, grad_cells[r * COLS : (r + 1) * COLS], 0.0)
        grad_columns = term if grad_columns is None else grad_columns + term
    grad_columns = grad_columns.astype(BF16)
    grad_pixels = None
    for k in range(4):
        term = dot_tn(
            grad_columns[:, 128 * k : 128 * k + 128], column_pick[32 * k : 32 * k + 32, :]
        )
        grad_pixels = term if grad_pixels is None else grad_pixels + term
    delta_grad[...] = grad_pixels[0:96].reshape(4, 24, 128)

    stem_low = dot_tn(patches, grad_pre)
    stem_low = jnp.concatenate([stem_low, jnp.zeros((16, C1), F32)], axis=0).astype(BF16)
    tap_low = tap_grad[...].astype(BF16)
    slots = []
    for stem_at, tap_at in ((2, 3), (6, 7)):
        slot = dot_nn(stem_low, one_hot(table[stem_at : stem_at + 1, 0:256], C1))
        slot = slot + dot_nn(tap_low, one_hot(table[tap_at : tap_at + 1, 0:256], C1))
        slots.append(slot)
    paired = jnp.concatenate(slots, axis=0).T
    small[...] = paired.reshape(4, NXH, NY, NZ, 128)
    core_small = core_start((small, c_small), (delta_grad, c_delta))

    settle(first_ds)
    first_sum(h_ds_lo, h_ds_hi, x_ds_lo, x_ds_hi, n_ds_lo, n_ds_hi)
    second_ds = second_start(n_ds_lo, n_ds_hi, y_ds_lo, y_ds_hi)

    settle(core_small)
    for lo in range(NXL):
        h_small[lo] = small[lo * NC + core] + c_small[lo]
        h_delta[lo] = delta_grad[lo * NC + core] + c_delta[lo]
    first_small = []
    for t in range(1, 4):
        other_hi, other_lo, peer = x_peer(t)
        first_small.append(ship(h_delta.at[other_lo], x_delta.at[x], peer))
        first_small.append(ship(h_small.at[other_lo, other_hi], x_small.at[t - 1], peer))
    x_delta[x] = h_delta[x_lo]

    settle(first_ud)
    first_sum(h_ud_lo, h_ud_hi, x_ud_lo, x_ud_hi, n_ud_lo, n_ud_hi)
    second_ud = second_start(n_ud_lo, n_ud_hi, y_ud_lo, y_ud_hi)

    settle(first_small)
    n_delta[...] = (x_delta[0] + x_delta[1]) + (x_delta[2] + x_delta[3])
    n_small[...] = (h_small[x_lo, x_hi] + x_small[0]) + (x_small[1] + x_small[2])
    second_small = []
    for t in range(1, 4):
        other, peer = y_peer(t)
        second_small.append(ship(n_delta, y_delta.at[y], peer))
        second_small.append(ship(n_small.at[other], y_small.at[t - 1], peer))
    y_delta[y] = n_delta[...]

    settle(second_ds)
    second_sum(n_ds_lo, n_ds_hi, y_ds_lo, y_ds_hi, rows_ds)
    stage[:, 12:16] = jnp.zeros((NZ, 4, WIDE), F32)
    for k in range(NZ):
        stage[k, 0:6] = rows_ds[6 * k : 6 * k + 6]
    settle(second_ud)
    second_sum(n_ud_lo, n_ud_hi, y_ud_lo, y_ud_hi, rows_ud)
    for k in range(NZ):
        stage[k, 6:12] = rows_ud[6 * k : 6 * k + 6]
    settle(second_small)
    rows_small[...] = (n_small[y] + y_small[0]) + (y_small[1] + y_small[2])
    for k in range(NZ):
        stage[k, 12:13, 0:128] = rows_small[k : k + 1]
    low[...] = stage[...].astype(BF16)
    low_delta[z] = ((y_delta[0] + y_delta[1]) + (y_delta[2] + y_delta[3])).astype(BF16)

    sent = []
    for t in range(1, NZ):
        other, peer = z_peer(t)
        sent.append(ship(low_delta.at[z], low_delta.at[z], peer))
        sent.append(ship(low.at[other], got_z.at[t - 1], peer))
    settle(sent)
    total = stage[z]
    for t in range(NZ - 1):
        total = total + got_z[t].astype(F32)
    shares[strip] = total
    total = low_delta[0].astype(F32)
    for k in range(1, NZ):
        total = total + low_delta[k].astype(F32)
    square = total * total
    for channel in range(3):
        misc[channel] = total[8 * channel : 8 * channel + 8]
    misc[4 + strip] = square[0:8] + square[8:16] + square[16:24]

    sent = []
    for t in range(1, 4):
        peer = (dp, strip_peer(t))
        sent.append(ship(shares.at[strip], shares.at[strip], peer))
        sent.append(ship(misc.at[4 + strip], misc.at[4 + strip], peer))
    settle(sent)


N_COPIES = 6 + 3 * 4 + 3 * 6 + 3 * 6 + 14 + 6
N_LOADS = 13


def finish_kernel(
    levels,
    shares,
    misc,
    perturbation,
    loss_out,
    new_out,
    stem_out,
    dw_out,
    up_out,
    down_out,
    ds_out,
    head_out,
):
    loss_out[0] = misc[3][0, 0]
    total = jnp.sum((misc[4] + misc[5]) + (misc[6] + misc[7]))
    spread = jnp.sqrt(jnp.full((8, 128), total, F32) * (1.0 / 12288) + EPS_ROOT)
    for channel in range(3):
        level = STEP_UNIT * levels[channel].astype(F32)
        step = level * misc[channel] / spread
        new_out[channel] = jnp.clip(perturbation[channel] + step, -BOUND, BOUND)
    up_out[0:6] = shares[0, 6:12, 0:C1]
    up_out[6:12] = shares[1, 6:12, 0:C1]
    down_out[0:6] = shares[2, 6:12, 0:C1]
    down_out[6:12] = shares[3, 6:12, 0:C1]
    for place in range(4):
        ds_out[:, place * C1 : (place + 1) * C1] = shares[place, 0:6, 0:C1]
    head_out[...] = shares[0, 0:6, C1 : C1 + CLASSES]
    stem_out[0:1] = shares[0, 12:13, 0:48]
    stem_out[1:2] = shares[0, 12:13, 64 : 64 + 48]
    stem_out[2:3] = shares[1, 12:13, 0:48]
    dw_out[0:1] = shares[1, 12:13, 64 : 64 + 49]
    dw_out[1:2] = shares[2, 12:13, 0:49]
    dw_out[2:3] = shares[2, 12:13, 64 : 64 + 49]


VMEM = pl.BlockSpec(memory_space=pltpu.VMEM)
SMEM = pl.BlockSpec(memory_space=pltpu.SMEM)
ANY = pl.BlockSpec(memory_space=pl.ANY)


def shaped(shape, dtype):
    return jax.ShapeDtypeStruct(shape, dtype)


def run_step(labels, head_gain, *operands):
    strips, parts = NXL * NC, (NXL, NXH, NY, PIECE, 128)

    def low_and_high(first, second):
        return [pltpu.VMEM(first, BF16), pltpu.VMEM(second, BF16)]

    f32 = lambda *shape: pltpu.VMEM(shape, F32)
    bf16 = lambda *shape: pltpu.VMEM(shape, BF16)
    lo, hi = (NXH, NY, PIECE, 128), (NY, NXH, PIECE, 128)
    scratch = [
        bf16(4, 3, 8, 128),
        f32(4, 3, 8, 128),
        pltpu.VMEM((8, F1), jnp.int32),
        bf16(48, C1),
        f32(1, C1),
        bf16(KS * KS, C1),
        f32(1, C1),
        bf16(C1, F1),
        bf16(C1, F1),
        f32(1, C1),
        f32(1, C1),
        bf16(4 * C1, C2),
        bf16(CLASSES, C2),
        f32(ROWS, COLS + 16, C1),
        f32(KS, ROWS, COLS, C1),
        f32(ROWS, COLS, C1),
        bf16(CELLS, WIDE),
        bf16(CELLS, WIDE),
        bf16(CELLS, WIDE),
        f32(64, C1),
        f32(KS * KS, C1),
        bf16(F1, F1),
        bf16(C2, C2),
    ]
    for count in (strips, NXL):
        scratch += [bf16(count, *lo), bf16(count, *hi)] * 2
        scratch += [f32(count, NXH, NY, NZ, 128), f32(count, 24, 128)]
    scratch += [bf16(NXL, *lo), bf16(NY, NXL, NXH, PIECE, 128)] * 2
    scratch += [f32(NXL, NXH, NY, NZ, 128), f32(NXL, 24, 128)]
    scratch += [bf16(3, NY, PIECE, 128), bf16(3, NXL, NXH, PIECE, 128)] * 2
    scratch += [f32(3, NY, NZ, 128), f32(NX, 24, 128)]
    scratch += [bf16(NY, PIECE, 128), bf16(NXL, NXH, PIECE, 128)] * 2
    scratch += [f32(NY, NZ, 128), f32(24, 128)]
    scratch += [bf16(3, PIECE, 128)] * 4 + [f32(3, NZ, 128), f32(NY, 24, 128)]
    scratch += [f32(PIECE, WIDE)] * 2 + [f32(NZ, 128)]
    scratch += [f32(NZ, 16, WIDE), bf16(NZ, 16, WIDE), bf16(NZ - 1, 16, WIDE), bf16(NZ, 24, 128)]
    scratch += [
        pltpu.SemaphoreType.DMA((N_LOADS,)),
        pltpu.SemaphoreType.DMA((N_COPIES,)),
        pltpu.SemaphoreType.DMA((N_COPIES,)),
    ]
    return pl.pallas_call(
        step_kernel,
        name="image_step_and_reduce",
        out_shape=(shaped((4, 16, WIDE), F32), shaped((8, 8, 128), F32)),
        in_specs=[SMEM, VMEM] + [ANY] * len(operands),
        out_specs=(VMEM, VMEM),
        scratch_shapes=scratch,
        compiler_params=pltpu.CompilerParams(
            collective_id=0, has_side_effects=True, vmem_limit_bytes=60 * 1024 * 1024
        ),
    )(labels, head_gain, *operands)


def run_finish(levels, shares, misc, perturbation):
    return pl.pallas_call(
        finish_kernel,
        name="finish",
        out_shape=(
            shaped((1,), F32),
            shaped((3, 8, 128), F32),
            shaped((3, 48), F32),
            shaped((3, KS * KS), F32),
            shaped((12, C1), F32),
            shaped((12, C1), F32),
            shaped((6, 4 * C1), F32),
            shaped((6, CLASSES), F32),
        ),
        in_specs=[SMEM] + [VMEM] * 3,
        out_specs=(SMEM,) + (VMEM,) * 7,
    )(levels, shares, misc, perturbation)


def on_device(
    images,
    perturbation,
    labels,
    step_levels,
    stem_weight,
    stem_gain,
    dw1_kernel,
    norm1_gain,
    up1_weight,
    down1_weight,
    scale1,
    down_gain,
    ds_weight,
    head_gain,
    head_weight,
):
    shares, misc = run_step(
        labels,
        head_gain,
        images,
        perturbation,
        jnp.asarray(index_table()),
        stem_weight,
        stem_gain.reshape(1, C1),
        dw1_kernel,
        norm1_gain.reshape(1, C1),
        up1_weight,
        down1_weight.T,
        scale1.reshape(1, C1),
        down_gain.reshape(1, C1),
        ds_weight,
        head_weight.T,
    )
    loss, new_delta, stem, dw, up, down, ds, head = run_finish(
        step_levels, shares, misc, perturbation
    )
    return (new_delta, loss, stem.T, dw.T, up.T, down, ds.T, head)


def solution(mesh):
    return jax.shard_map(
        on_device,
        mesh=mesh,
        in_specs=(
            P("dp", None, "strip", None),
            P(None, "strip", None),
            P(("dp", "strip")),
        )
        + (P(),) * 12,
        out_specs=(
            P(None, "strip", None),
            P(("dp", "strip")),
            P(None, "dp"),
            P(None, "dp"),
            P(None, "dp"),
            P("dp", None),
            P(None, "dp"),
            P("dp", None),
        ),
        check_vma=False,
    )
```

time: 67.3 us -> 45.7 us (0.68)
  local copies, waits for them, and re-layouts: 14.4 us -> 0 us
  Pallas kernels: 50.7 us -> 44.3 us
    unnamed x36 -> x0, local copies, waits for them, and re-layouts: 13.7 us -> none
    pallas_call x4 -> x2, Pallas kernels: 50.7 us -> 44.3 us  [the longest x1 42.6 us: run_step(): pl.pallas_call(step_kernel, name='image_step_and_reduce', out_shape=(shap...]
    reshape x1 -> x0, local copies, waits for them, and re-layouts: 0.68 us -> none  [on_device(): head_gain.reshape(1, C2)]
where the time goes in v2:
time: 45.7 us; the launch traced here: 45.5 us
  Pallas kernels  44.3 us (97%)
  between operations  1.29 us (3%)
    pallas_call x1, Pallas kernels, run_step(): pl.pallas_call(step_kernel, name='image_step_and_reduce', out_shape=(shap...  42.6 us
    pallas_call x1, Pallas kernels, run_finish(): pl.pallas_call(finish_kernel, name='finish', out_shape=(shaped((1,), F32)...  1.63 us

profile of v2, /device:TPU:1, one launch (start us, length us, event | category | flops | bytes accessed | tf_op | source)
XLA Modules:
  0.0 45.5 jit_solution(488575490497678294)
XLA Ops:
  1.3 42.6 %image_step_and_reduce.1 = (f32[4,16,256]{2,1,0:T(8,128)}, f32[8,8,128]{2,1,0:T(8,128)}) custom-call(s32[1]{0:T(128)S(6)} %copy.24.label, f32[384]{0:T(512)} %head_gain.1, bf16[4,3,8,128]{3,2,1,0:T(8,128)(2,1)} %images.1, f32[3,8,128]{2,1,0:T(8,128)} %perturbation.1, s32[8,768]{1,0:T(8,128)} %constant.2.clone.table_in, bf16[48,192]{1,0:T(8,128)(2,1)} %stem_in.1, ...), custom_call_target="tpu_custom_call" | custom-call | tf_op jit(solution)/shard_map/image_step_and_reduce/pallas_call | solution.py:685
  43.9 1.6 %finish.1 = (f32[1]{0:T(128)}, f32[3,8,128]{2,1,0:T(8,128)}, f32[3,48]{1,0:T(4,128)}, f32[3,49]{1,0:T(4,128)}, f32[12,192]{1,0:T(8,128)}, /*index=5*/f32[12,192]{1,0:T(8,128)}, f32[6,768]{1,0:T(8,128)}, f32[6,62]{1,0:T(8,128)}) custom-call(s32[3]{0:T(128)} %levels.1, f32[4,16,256]{2,1,0:T(8,128)} %get-tuple-element.18.shares, ...), custom_call_target="tpu_custom_call" | custom-call | tf_op jit(solution)/shard_map/finish/pallas_call | solution.py:699

commit v3 on v2

v3 whole, which is shorter than its diff:
```python
import jax
import jax.numpy as jnp
import numpy as np
from jax import lax
from jax.experimental import pallas as pl
from jax.experimental.pallas import tpu as pltpu
from jax.sharding import PartitionSpec as P

KS = 7
EPS_NORM = 1e-06
EPS_ROOT = 1e-12
BOUND = 0.5
STEP_UNIT = 0.1

NZ, NY, NXH, NXL, NC = 8, 4, 2, 2, 2
NX = NXH * NXL
ROWS, COLS, CELLS = 8, 32, 256
C1, F1, C2, CLASSES = 192, 768, 384, 62
WIDE = 256
PIECE = 48

F32 = jnp.float32
BF16 = jnp.bfloat16
MESH = pl.DeviceIdType.MESH


def index_table():
    table = np.full((16, F1), -1, np.int32)
    slots = {(0, 0): (2, 0), (0, 1): (6, 1), (1, 0): (2, 2), (1, 1): (7, 0), (2, 0): (3, 1), (2, 1): (7, 2)}
    for x_hi in range(NXH):
        for y in range(NY):
            for z in range(NZ):
                own = (z * NY + y) * NXH + x_hi
                block = (x_hi * NY + y) * NZ + z
                for q in range(6):
                    table[0, 6 * block + q] = own * 12 + q
                    table[0, 384 + 6 * block + q] = own * 12 + 6 + q
                    table[1, 6 * block + q] = own * 6 + q
                    table[8, 6 * block + q] = x_hi * NY + y
                    table[9, 6 * block + q] = 64 + z * 6 + q
                for (strip, _), (row, column) in slots.items():
                    table[row, strip * 64 + block] = own * 3 + column
    for part_col in range(4):
        for strip in range(4):
            for channel in range(3):
                for row in range(8):
                    lane = part_col * 128 + strip * 24 + channel * 8 + row
                    table[4, lane] = channel * 16 + (row % 4) * 4 + part_col
                    table[5, lane] = strip * 2 + row // 4
    return table


def dot_nn(a, b):
    return lax.dot_general(a, b, (((1,), (0,)), ((), ())), preferred_element_type=F32)


def dot_nt(a, b):
    return lax.dot_general(a, b, (((1,), (1,)), ((), ())), preferred_element_type=F32)


def dot_tn(a, b):
    return lax.dot_general(a, b, (((0,), (0,)), ((), ())), preferred_element_type=F32)


def mean_lanes(values):
    return jnp.sum(values, axis=-1, keepdims=True) * (1.0 / values.shape[-1])


def norm_parts(values):
    centred = values - mean_lanes(values)
    root = lax.rsqrt(mean_lanes(centred * centred) + EPS_NORM)
    return centred * root, root


def norm_back(unit, root, grad):
    return root * (grad - mean_lanes(grad) - unit * mean_lanes(grad * unit))


def one_hot(index_row, rows):
    width = index_row.shape[1]
    return (lax.broadcasted_iota(jnp.int32, (rows, width), 0) == index_row).astype(F32).astype(BF16)


def step_kernel(
    label_in,
    head_gain_in,
    images,
    strip_delta,
    table_in,
    stem_in,
    stem_gain_in,
    taps_in,
    norm1_in,
    up_in,
    down_in,
    scale_in,
    down_gain_in,
    ds_in,
    head_in_t,
    shares,
    misc,
    label,
    head_gain,
    own_images,
    own_delta,
    own_pixels,
    pixels,
    table,
    stem_weight,
    stem_gain,
    taps,
    norm1_gain,
    up_weight,
    down_weight,
    scale1,
    down_gain,
    ds_weight,
    head_weight,
    padded,
    shifted,
    mixed_ref,
    wide_merged,
    wide_normed,
    wide_branch,
    tap_grad,
    taps_ref,
    up_ordered,
    down_ordered,
    unit_pick,
    column_pick,
    feature_pick,
    fold,
    slot_pick,
    factors,
    ud,
    small,
    delta_grad,
    c_ud,
    c_small,
    c_delta,
    h_ud,
    h_late,
    got_factors,
    x_ud,
    x_late,
    rows_ds,
    rows_ud,
    rows_late,
    stage,
    low,
    got_z,
    low_delta,
    local,
    send,
    recv,
):
    dp, strip = lax.axis_index("dp"), lax.axis_index("strip")
    z, y, x_hi = dp // (NY * NXH), (dp // NXH) % NY, dp % NXH
    x_lo, core = strip // NC, strip % NC
    x = x_hi * NXL + x_lo

    plane_steps = sorted(
        ((i, j) for i in range(NX) for j in range(NY) if i or j),
        key=lambda step: -(min(step[0], NX - step[0]) + min(step[1], NY - step[1])),
    )

    def plane_peer(step):
        other, other_y = (x + step[0]) % NX, (y + step[1]) % NY
        other_hi, other_lo = other // NXL, other % NXL
        other_dp = (z * NY + other_y) * NXH + other_hi
        same, crossed = (other_dp, other_lo * NC + core), (other_dp, other_lo * NC + 1 - core)
        return other_lo, other_hi, other_y, same, crossed

    def z_peer(t):
        other = (z + t) % NZ
        return other, ((other * NY + y) * NXH + x_hi, strip)

    def strip_peer(t):
        return (strip + t) % (NXL * NC)

    barrier = pltpu.get_barrier_semaphore()
    peers = [(dp, strip_peer(t)) for t in range(1, 4)]
    peers += [plane_peer(step)[3] for step in plane_steps]
    peers += [plane_peer(step)[4] for step in plane_steps]
    peers += [z_peer(t)[1] for t in range(1, NZ)]
    for peer in peers:
        pl.semaphore_signal(barrier, inc=1, device_id=peer, device_id_type=MESH)

    loads = {}
    for k, (name, source, target) in enumerate(
        (
            ("images", images, own_images),
            ("delta", strip_delta, own_delta),
            ("table", table_in, table),
            ("label", label_in, label),
            ("head_gain", head_gain_in, head_gain),
            ("stem", stem_in, stem_weight),
            ("stem_gain", stem_gain_in, stem_gain),
            ("taps", taps_in, taps),
            ("norm1", norm1_in, norm1_gain),
            ("up", up_in, up_weight),
            ("down", down_in, down_weight),
            ("scale", scale_in, scale1),
            ("down_gain", down_gain_in, down_gain),
            ("ds", ds_in, ds_weight),
            ("head", head_in_t, head_weight),
        )
    ):
        loads[name] = pltpu.make_async_copy(source, target, local.at[k])
        loads[name].start()

    count = [0]

    def ship(source, target, peer):
        k = count[0]
        count[0] += 1
        copy = pltpu.make_async_remote_copy(
            src_ref=source,
            dst_ref=target,
            send_sem=send.at[k],
            recv_sem=recv.at[k],
            device_id=peer,
            device_id_type=MESH,
        )
        copy.start()
        return copy

    def settle(copies):
        for copy in copies:
            copy.wait()

    wide_merged[...] = jnp.zeros((CELLS, WIDE), BF16)
    wide_normed[...] = jnp.zeros((CELLS, WIDE), BF16)
    wide_branch[...] = jnp.zeros((CELLS, WIDE), BF16)
    tap_grad[...] = jnp.zeros_like(tap_grad)
    padded[:, 0:8, :] = jnp.zeros((ROWS, 8, C1), F32)
    padded[:, 8 + COLS :, :] = jnp.zeros((ROWS, 8, C1), F32)
    loads["table"].wait()
    hidden_pick = one_hot(table[0:1, :], F1)
    loads["up"].wait()
    up_ordered[...] = dot_nn(up_weight[...], hidden_pick).astype(BF16)
    loads["down"].wait()
    down_ordered[...] = dot_nn(down_weight[...], hidden_pick).astype(BF16)
    unit_pick[...] = one_hot(table[1:2, 0:C2], C2)
    feature_pick[...] = one_hot(table[4:5, 0:512], 48)
    fold[...] = one_hot(table[9:10, 0:C2], 128)
    for k, row in enumerate((2, 3, 6, 7)):
        slot_pick[k] = one_hot(table[row : row + 1, 0:256], C1)
    i0 = lax.broadcasted_iota(jnp.int32, (128, 128), 0)
    i1 = lax.broadcasted_iota(jnp.int32, (128, 128), 1)
    column_pick[...] = (i1 == 4 * (i0 & 31) + (i0 >> 5)).astype(F32).astype(BF16)
    loads["taps"].wait()
    taps_ref[...] = taps[...].astype(F32)
    loads["images"].wait()
    loads["delta"].wait()
    own_pixels[...] = (own_images[...].astype(F32) + own_delta[...]).astype(BF16)
    pl.semaphore_wait(barrier, len(peers))

    sent = []
    for t in range(1, 4):
        peer = strip_peer(t)
        sent.append(ship(own_pixels.at[peer], pixels.at[strip], (dp, peer)))
    pixels[strip] = own_pixels[strip]
    for name in (
        "label", "head_gain", "stem", "stem_gain", "norm1", "scale", "down_gain", "ds", "head"
    ):
        loads[name].wait()
    settle(sent)

    perturbed = pixels[...].astype(F32).reshape(96, 128)
    perturbed = jnp.concatenate([perturbed, jnp.zeros((32, 128), F32)], axis=0).astype(BF16)
    columns = dot_nt(column_pick[...], perturbed)
    columns = jnp.concatenate([columns[32 * k : 32 * k + 32] for k in range(4)], axis=1)
    row_of = table[5:6, 0:512]
    cells = jnp.concatenate(
        [jnp.where(row_of == r, columns, 0.0) for r in range(ROWS)], axis=0
    ).astype(BF16)
    patches = dot_nt(cells, feature_pick[...]).astype(BF16)

    stem_pre = dot_nn(patches, stem_weight[...])
    stem_unit, stem_root = norm_parts(stem_pre)
    stem_out = (stem_unit * stem_gain[...]).astype(BF16).astype(F32)

    def spread_columns(values):
        padded[:, 8 : 8 + COLS, :] = values.reshape(ROWS, COLS, C1)
        for j in range(KS):
            shifted[j] = padded[:, 5 + j : 5 + j + COLS, :]

    def correlate(tap_of):
        for r in range(ROWS):
            total = None
            for i in range(KS):
                if 0 <= r + i - 3 < ROWS:
                    for j in range(KS):
                        tap = tap_of(i, j)
                        term = shifted[j, r + i - 3] * taps_ref[tap : tap + 1, :]
                        total = term if total is None else total + term
            mixed_ref[r] = total
        return mixed_ref[...].reshape(CELLS, C1)

    spread_columns(stem_out)
    mixed = correlate(lambda i, j: KS * i + j)

    mixed_unit, mixed_root = norm_parts(mixed)
    normed = (mixed_unit * norm1_gain[...]).astype(BF16)
    wide_normed[:, 0:C1] = normed
    upper = dot_nn(normed, up_ordered[...])
    half = 0.5 + 0.5 * lax.erf(upper * (0.5**0.5))
    hidden = (upper * half).astype(BF16)
    gelu_slope = half + upper * jnp.exp(-0.5 * upper * upper) * ((2.0 * np.pi) ** -0.5)
    branch = dot_nt(hidden, down_ordered[...])
    section = (stem_out + scale1[...] * branch).astype(BF16).astype(F32)

    section_unit, section_root = norm_parts(section)
    wide_merged[:, 0:C1] = (section_unit * down_gain[...]).astype(BF16)
    p0 = lax.broadcasted_iota(jnp.int32, (16, CELLS), 0)
    p1 = lax.broadcasted_iota(jnp.int32, (16, CELLS), 1)
    place_pick = (p0 == 2 * ((p1 >> 5) & 1) + (p1 & 1)).astype(F32).astype(BF16)
    merged_sum = dot_nn(place_pick, wide_merged[...])
    sums_high = merged_sum.astype(BF16).astype(F32)
    rest = merged_sum - sums_high
    sums_mid = rest.astype(BF16).astype(F32)
    sums_low = rest - sums_mid
    row16 = lax.broadcasted_iota(jnp.int32, (16, WIDE), 0)

    def place_rows(place):
        high = sums_high[place : place + 1]
        mid = sums_mid[place : place + 1]
        lowest = sums_low[place : place + 1]
        return jnp.where(
            row16 == 0, high, jnp.where(row16 == 1, mid, jnp.where(row16 == 2, lowest, 0.0))
        ).astype(BF16)

    split_sums = [place_rows(place) for place in range(4)]
    pooled = None
    for place in range(4):
        term = dot_nn(split_sums[place][:, 0:C1], ds_weight[place * C1 : (place + 1) * C1, :])
        pooled = term if pooled is None else pooled + term
    cells_two = CELLS // 4
    pooled = jnp.sum(pooled, axis=0, keepdims=True) * (1.0 / cells_two)
    pooled = jnp.broadcast_to(pooled, (16, C2))
    head_unit, head_root = norm_parts(pooled)
    gain = head_gain[...].reshape(1, C2)
    head_in = (head_unit * gain).astype(BF16)
    logits = dot_nt(head_in, head_weight[...])
    onehot = (lax.broadcasted_iota(jnp.int32, logits.shape, 1) == label[0]).astype(F32)
    top = jnp.max(logits, axis=-1, keepdims=True)
    raised = jnp.exp(logits - top)
    mass = jnp.sum(raised, axis=-1, keepdims=True)
    losses = jnp.log(mass) + top - jnp.sum(onehot * logits, axis=-1, keepdims=True)
    misc[3] = jnp.broadcast_to(losses[0:8], (8, 128))
    grad_logits = (raised / mass - onehot).astype(BF16)
    grad_head_in = dot_nn(grad_logits, head_weight[...])
    grad_pooled = norm_back(head_unit, head_root, grad_head_in * gain)
    grad_start = (grad_pooled * (1.0 / cells_two)).astype(BF16)

    block_of = lax.broadcasted_iota(jnp.int32, (16, C2), 0) == table[8:9, 0:C2]
    start_rows = jnp.where(block_of, dot_nn(grad_start, unit_pick[...]), 0.0).astype(BF16)
    start_blocks = dot_nt(start_rows, fold[...])
    head_rows = jnp.where(block_of, dot_nn(head_in, unit_pick[...]), 0.0).astype(BF16)
    head_blocks = dot_nt(head_rows, fold[...])
    e0 = lax.broadcasted_iota(jnp.int32, (CLASSES, 128), 0)
    e1 = lax.broadcasted_iota(jnp.int32, (CLASSES, 128), 1)
    logit_row = dot_nn(grad_logits, (e0 == e1).astype(F32).astype(BF16))[0:1]
    row8 = lax.broadcasted_iota(jnp.int32, (8, 128), 0)
    for hi in range(NXH):
        for k in range(NY):
            at = hi * NY + k
            third = jnp.where(row8 == 2, logit_row + head_blocks[at : at + 1], 0.0)
            for place in range(4):
                second = merged_sum[place : place + 1, 128:256] + start_blocks[at : at + 1]
                first = merged_sum[place : place + 1, 0:128]
                factors[place, hi, k] = jnp.where(row8 == 0, first, jnp.where(row8 == 1, second, third))
    mine = (x * NY + y) * NC + core
    factor_copies = []
    for step in plane_steps:
        other_lo, other_hi, other_y, same, crossed = plane_peer(step)
        for other_core, peer in ((core, same), (1 - core, crossed)):
            source = factors.at[other_lo * NC + other_core, other_hi, other_y]
            factor_copies.append(ship(source, got_factors.at[mine], peer))
    partner = (dp, x_lo * NC + (1 - core))
    source = factors.at[x_lo * NC + (1 - core), x_hi, y]
    factor_copies.append(ship(source, got_factors.at[mine], partner))
    got_factors[mine] = factors[strip, x_hi, y]

    def store_rows(blocks, at_strip, grads):
        for hi in range(NXH):
            for k in range(NY):
                at = (hi * NY + k) * PIECE
                blocks[at_strip, hi, k] = grads[at : at + PIECE].astype(BF16)

    def core_start(*pairs):
        copies = []
        for lo in range(NXL):
            for source, target in pairs:
                copies.append(ship(source.at[lo * NC + (1 - core)], target.at[lo], partner))
        return copies

    def core_sum(own, got, held):
        for lo in range(NXL):
            block = own[lo * NC + core].astype(F32) + got[lo].astype(F32)
            held[lo] = block.astype(BF16)

    def plane_start(held, got):
        copies = []
        for k, step in enumerate(plane_steps):
            other_lo, other_hi, other_y, peer, _ = plane_peer(step)
            copies.append(ship(held.at[other_lo, other_hi, other_y], got.at[k], peer))
        return copies

    def plane_sum(held, got, rows):
        total = held[x_lo, x_hi, y].astype(F32)
        for k in range(len(plane_steps)):
            total = total + got[k].astype(F32)
        rows[...] = total

    place_grads = [
        dot_nt(grad_start, ds_weight[place * C1 : (place + 1) * C1, :])[0:1] * down_gain[...]
        for place in range(4)
    ]
    even = (lax.broadcasted_iota(jnp.int32, (COLS, C1), 0) & 1) == 0
    by_row = [
        jnp.where(even, place_grads[2 * k], place_grads[2 * k + 1]) for k in range(2)
    ]
    grad_unit = jnp.concatenate([by_row[r % 2] for r in range(ROWS)], axis=0)
    grad_block = norm_back(section_unit, section_root, grad_unit).astype(BF16).astype(F32)

    grad_branch = (grad_block * scale1[...]).astype(BF16)
    wide_branch[:, 0:C1] = grad_branch
    grad_down = dot_tn(hidden, wide_branch[...])
    store_rows(ud, 2, grad_down[0:384])
    store_rows(ud, 3, grad_down[384:768])
    grad_hidden = dot_nn(grad_branch, down_ordered[...])
    grad_upper = (grad_hidden * gelu_slope).astype(BF16)
    grad_up = dot_tn(grad_upper, wide_normed[...])
    store_rows(ud, 0, grad_up[0:384])
    store_rows(ud, 1, grad_up[384:768])
    core_ud = core_start((ud, c_ud))

    grad_normed = dot_nt(grad_upper, up_ordered[...])
    grad_mixed = norm_back(mixed_unit, mixed_root, grad_normed * norm1_gain[...])

    mixed_ref[...] = grad_mixed.reshape(ROWS, COLS, C1)
    for i in range(KS):
        for j in range(KS):
            total = None
            for r in range(ROWS):
                if 0 <= r + i - 3 < ROWS:
                    term = shifted[j, r + i - 3] * mixed_ref[r]
                    total = term if total is None else total + term
            tap = KS * i + j
            tap_grad[tap : tap + 1, :] = jnp.sum(total, axis=0, keepdims=True)

    settle(core_ud)
    core_sum(ud, c_ud, h_ud)
    plane_ud = plane_start(h_ud, x_ud)

    spread_columns(grad_mixed)
    grad_stem = grad_block + correlate(lambda i, j: KS * (KS - 1 - i) + (KS - 1 - j))
    grad_pre = norm_back(stem_unit, stem_root, grad_stem * stem_gain[...]).astype(BF16)

    grad_patches = dot_nt(grad_pre, stem_weight[...]).astype(BF16)
    grad_cells = dot_nn(grad_patches, feature_pick[...])
    grad_columns = None
    for r in range(ROWS):
        term = jnp.where(row_of == r, grad_cells[r * COLS : (r + 1) * COLS], 0.0)
        grad_columns = term if grad_columns is None else grad_columns + term
    grad_columns = grad_columns.astype(BF16)
    grad_pixels = None
    for k in range(4):
        term = dot_tn(
            grad_columns[:, 128 * k : 128 * k + 128], column_pick[32 * k : 32 * k + 32, :]
        )
        grad_pixels = term if grad_pixels is None else grad_pixels + term
    delta_grad[...] = grad_pixels[0:96].reshape(4, 24, 128).astype(BF16)

    stem_low = dot_tn(patches, grad_pre)
    stem_low = jnp.concatenate([stem_low, jnp.zeros((16, C1), F32)], axis=0).astype(BF16)
    tap_low = tap_grad[...].astype(BF16)
    slots = []
    for k in range(2):
        slots.append(dot_nn(stem_low, slot_pick[2 * k]) + dot_nn(tap_low, slot_pick[2 * k + 1]))
    paired = jnp.concatenate(slots, axis=0).T
    small[...] = paired.reshape(4, NXH, NY, NZ, 128)
    core_small = core_start((small, c_small), (delta_grad, c_delta))

    settle(core_small)
    for lo in range(NXL):
        mine = lo * NC + core
        block = delta_grad[mine].astype(F32) + c_delta[lo].astype(F32)
        late = small[mine] + c_small[lo]
        for hi in range(NXH):
            for k in range(NY):
                h_late[lo, hi, k] = jnp.concatenate([block, late[hi, k]], axis=0).astype(BF16)
    plane_late = []
    mine = x * NY + y
    for step in plane_steps:
        other_lo, other_hi, other_y, peer, _ = plane_peer(step)
        plane_late.append(ship(h_late.at[other_lo, other_hi, other_y], x_late.at[mine], peer))
    x_late[mine] = h_late[x_lo, x_hi, y]

    settle(factor_copies)
    low_half, high_half = got_factors[:, 0, :], got_factors[:, 1, :]
    third = got_factors[:, 2, :]
    first_lanes = lax.broadcasted_iota(jnp.int32, high_half.shape, 1) < 64
    sums = jnp.concatenate([low_half, jnp.where(first_lanes, high_half, 0.0)], axis=1)
    sums_high = sums.astype(BF16)
    sums_low = (sums - sums_high.astype(F32)).astype(BF16)
    starts = high_half.astype(BF16)
    o0 = lax.broadcasted_iota(jnp.int32, (128, WIDE), 0)
    o1 = lax.broadcasted_iota(jnp.int32, (128, WIDE), 1)
    head_offset = ((o1 == o0 + C1) & (o0 < 64)).astype(F32).astype(BF16)
    third = third.astype(BF16)
    placed_logits = dot_nn(third, head_offset).astype(BF16)
    products = dot_tn(starts, sums_high) + dot_tn(starts, sums_low) + dot_tn(third, placed_logits)
    rows_ds[...] = products[64 : 64 + PIECE]
    stage[:, 12:16] = jnp.zeros((NZ, 4, WIDE), F32)
    for k in range(NZ):
        stage[k, 0:6] = rows_ds[6 * k : 6 * k + 6]
    settle(plane_ud)
    plane_sum(h_ud, x_ud, rows_ud)
    for k in range(NZ):
        stage[k, 6:12] = rows_ud[6 * k : 6 * k + 6]
    settle(plane_late)
    total = x_late[0].astype(F32)
    for k in range(1, NX * NY):
        total = total + x_late[k].astype(F32)
    rows_late[...] = total[24:32]
    low_delta[z] = total[0:24].astype(BF16)
    for k in range(NZ):
        stage[k, 12:13, 0:128] = rows_late[k : k + 1]
    low[...] = stage[...].astype(BF16)

    sent = []
    for t in range(1, NZ):
        other, peer = z_peer(t)
        sent.append(ship(low_delta.at[z], low_delta.at[z], peer))
        sent.append(ship(low.at[other], got_z.at[t - 1], peer))
    settle(sent)
    total = stage[z]
    for t in range(NZ - 1):
        total = total + got_z[t].astype(F32)
    shares[strip] = total.astype(BF16)
    total = low_delta[0].astype(F32)
    for k in range(1, NZ):
        total = total + low_delta[k].astype(F32)
    square = total * total
    for channel in range(3):
        misc[channel] = total[8 * channel : 8 * channel + 8]
    misc[4 + strip] = square[0:8] + square[8:16] + square[16:24]

    sent = []
    for t in range(1, 4):
        peer = (dp, strip_peer(t))
        sent.append(ship(shares.at[strip], shares.at[strip], peer))
        sent.append(ship(misc.at[4 + strip], misc.at[4 + strip], peer))
    settle(sent)


N_COPIES = 3 + 31 + 2 + 4 + 2 * 15 + 14 + 6
N_LOADS = 15


def finish_kernel(
    levels,
    shares,
    misc,
    perturbation,
    loss_out,
    new_out,
    stem_out,
    dw_out,
    up_out,
    down_out,
    ds_out,
    head_out,
):
    loss_out[0] = misc[3][0, 0]
    share = [shares[place].astype(F32) for place in range(4)]
    total = jnp.sum((misc[4] + misc[5]) + (misc[6] + misc[7]))
    spread = jnp.sqrt(jnp.full((8, 128), total, F32) * (1.0 / 12288) + EPS_ROOT)
    for channel in range(3):
        level = STEP_UNIT * levels[channel].astype(F32)
        step = level * misc[channel] / spread
        new_out[channel] = jnp.clip(perturbation[channel] + step, -BOUND, BOUND)
    up_out[0:6] = share[0][6:12, 0:C1]
    up_out[6:12] = share[1][6:12, 0:C1]
    down_out[0:6] = share[2][6:12, 0:C1]
    down_out[6:12] = share[3][6:12, 0:C1]
    for place in range(4):
        ds_out[:, place * C1 : (place + 1) * C1] = share[place][0:6, 0:C1]
    head_out[...] = share[0][0:6, C1 : C1 + CLASSES]
    stem_out[0:1] = share[0][12:13, 0:48]
    stem_out[1:2] = share[0][12:13, 64 : 64 + 48]
    stem_out[2:3] = share[1][12:13, 0:48]
    dw_out[0:1] = share[1][12:13, 64 : 64 + 49]
    dw_out[1:2] = share[2][12:13, 0:49]
    dw_out[2:3] = share[2][12:13, 64 : 64 + 49]


VMEM = pl.BlockSpec(memory_space=pltpu.VMEM)
SMEM = pl.BlockSpec(memory_space=pltpu.SMEM)
ANY = pl.BlockSpec(memory_space=pl.ANY)


def shaped(shape, dtype):
    return jax.ShapeDtypeStruct(shape, dtype)


def run_step(*operands):
    strips = NXL * NC
    f32 = lambda *shape: pltpu.VMEM(shape, F32)
    bf16 = lambda *shape: pltpu.VMEM(shape, BF16)
    scratch = [
        pltpu.SMEM((1,), jnp.int32),
        f32(C2),
        bf16(4, 3, 8, 128),
        f32(3, 8, 128),
        bf16(4, 3, 8, 128),
        bf16(4, 3, 8, 128),
        pltpu.VMEM((16, F1), jnp.int32),
        bf16(48, C1),
        f32(1, C1),
        bf16(KS * KS, C1),
        f32(1, C1),
        bf16(C1, F1),
        bf16(C1, F1),
        f32(1, C1),
        f32(1, C1),
        bf16(4 * C1, C2),
        bf16(CLASSES, C2),
        f32(ROWS, COLS + 16, C1),
        f32(KS, ROWS, COLS, C1),
        f32(ROWS, COLS, C1),
        bf16(CELLS, WIDE),
        bf16(CELLS, WIDE),
        bf16(CELLS, WIDE),
        f32(64, C1),
        f32(KS * KS, C1),
        bf16(C1, F1),
        bf16(C1, F1),
        bf16(C2, C2),
        bf16(128, 128),
        bf16(48, 512),
        bf16(128, C2),
        bf16(4, C1, 256),
    ]
    plane = NX * NY
    scratch += [f32(strips, NXH, NY, 8, 128)]
    for count in (strips, NXL):
        scratch += [bf16(count, NXH, NY, PIECE, WIDE)]
        scratch += [f32(count, NXH, NY, NZ, 128), bf16(count, 24, 128)]
    scratch += [bf16(NXL, NXH, NY, PIECE, WIDE), bf16(NXL, NXH, NY, 32, 128)]
    scratch += [f32(plane * NC, 8, 128), bf16(plane - 1, PIECE, WIDE), bf16(plane, 32, 128)]
    scratch += [f32(PIECE, WIDE)] * 2 + [f32(NZ, 128)]
    scratch += [f32(NZ, 16, WIDE), bf16(NZ, 16, WIDE), bf16(NZ - 1, 16, WIDE), bf16(NZ, 24, 128)]
    scratch += [
        pltpu.SemaphoreType.DMA((N_LOADS,)),
        pltpu.SemaphoreType.DMA((N_COPIES,)),
        pltpu.SemaphoreType.DMA((N_COPIES,)),
    ]
    return pl.pallas_call(
        step_kernel,
        name="image_step_and_reduce",
        out_shape=(shaped((4, 16, WIDE), BF16), shaped((8, 8, 128), F32)),
        in_specs=[ANY] * len(operands),
        out_specs=(VMEM, VMEM),
        scratch_shapes=scratch,
        compiler_params=pltpu.CompilerParams(
            collective_id=0, has_side_effects=True, vmem_limit_bytes=60 * 1024 * 1024
        ),
    )(*operands)


def run_finish(levels, shares, misc, perturbation):
    return pl.pallas_call(
        finish_kernel,
        name="finish",
        out_shape=(
            shaped((1,), F32),
            shaped((3, 8, 128), F32),
            shaped((3, 48), F32),
            shaped((3, KS * KS), F32),
            shaped((12, C1), F32),
            shaped((12, C1), F32),
            shaped((6, 4 * C1), F32),
            shaped((6, CLASSES), F32),
        ),
        in_specs=[SMEM] + [VMEM] * 3,
        out_specs=(SMEM,) + (VMEM,) * 7,
    )(levels, shares, misc, perturbation)


def on_device(
    images,
    perturbation,
    labels,
    step_levels,
    stem_weight,
    stem_gain,
    dw1_kernel,
    norm1_gain,
    up1_weight,
    down1_weight,
    scale1,
    down_gain,
    ds_weight,
    head_gain,
    head_weight,
):
    shares, misc = run_step(
        labels,
        head_gain,
        images,
        perturbation,
        jnp.asarray(index_table()),
        stem_weight,
        stem_gain.reshape(1, C1),
        dw1_kernel,
        norm1_gain.reshape(1, C1),
        up1_weight,
        down1_weight.T,
        scale1.reshape(1, C1),
        down_gain.reshape(1, C1),
        ds_weight,
        head_weight.T,
    )
    loss, new_delta, stem, dw, up, down, ds, head = run_finish(
        step_levels, shares, misc, perturbation
    )
    return (new_delta, loss, stem.T, dw.T, up.T, down, ds.T, head)


def solution(mesh):
    return jax.shard_map(
        on_device,
        mesh=mesh,
        in_specs=(
            P("dp", None, "strip", None),
            P(None, "strip", None),
            P(("dp", "strip")),
        )
        + (P(),) * 12,
        out_specs=(
            P(None, "strip", None),
            P(("dp", "strip")),
            P(None, "dp"),
            P(None, "dp"),
            P(None, "dp"),
            P("dp", None),
            P(None, "dp"),
            P("dp", None),
        ),
        check_vma=False,
    )
```

time: 45.7 us -> 42.2 us (0.923)
  Pallas kernels: 44.3 us -> 40.7 us
    pallas_call x1, Pallas kernels: 42.6 us -> 39.2 us  [run_step(): pl.pallas_call(step_kernel, name='image_step_and_reduce', out_shape=(shap...]
where the time goes in v3:
time: 42.2 us; the launch traced here: 42 us
  Pallas kernels  40.7 us (96%)
  between operations  1.29 us (3%)
    pallas_call x1, Pallas kernels, run_step(): pl.pallas_call(step_kernel, name='image_step_and_reduce', out_shape=(shap...  39.2 us
    pallas_call x1, Pallas kernels, run_finish(): pl.pallas_call(finish_kernel, name='finish', out_shape=(shaped((1,), F32)...  1.56 us

profile of v3, /device:TPU:1, one launch (start us, length us, event | category | flops | bytes accessed | tf_op | source)
XLA Modules:
  0.0 42.0 jit_solution(4892791425599848930)
XLA Ops:
  1.3 39.2 %image_step_and_reduce.1 = (bf16[4,16,256]{2,1,0:T(8,128)(2,1)}, f32[8,8,128]{2,1,0:T(8,128)}) custom-call(s32[1]{0:T(128)S(6)} %copy.24.label_in, f32[384]{0:T(512)} %head_gain_in.1, bf16[4,3,8,128]{3,2,1,0:T(8,128)(2,1)} %images.1, f32[3,8,128]{2,1,0:T(8,128)} %perturbation.1, s32[16,768]{1,0:T(8,128)} %constant.2.clone.table_in, bf16[48,192]{1,0:T(8,128)(2,1)} %stem_in.1, ...), custom_call_target="tpu_custom_call" | custom-call | tf_op jit(solution)/shard_map/image_step_and_reduce/pallas_call | solution.py:662
  40.4 1.6 %finish.1 = (f32[1]{0:T(128)}, f32[3,8,128]{2,1,0:T(8,128)}, f32[3,48]{1,0:T(4,128)}, f32[3,49]{1,0:T(4,128)}, f32[12,192]{1,0:T(8,128)}, /*index=5*/f32[12,192]{1,0:T(8,128)}, f32[6,768]{1,0:T(8,128)}, f32[6,62]{1,0:T(8,128)}) custom-call(s32[3]{0:T(128)} %levels.1, bf16[4,16,256]{2,1,0:T(8,128)(2,1)} %get-tuple-element.18.shares, ...), custom_call_target="tpu_custom_call" | custom-call | tf_op jit(solution)/shard_map/finish/pallas_call | solution.py:676

commit v4 on v3

--- a/solution.py
+++ b/solution.py
@@ -18,6 +18,7 @@
 C1, F1, C2, CLASSES = 192, 768, 384, 62
 WIDE = 256
 PIECE = 48
+FOLDED = 72
 
 F32 = jnp.float32
 BF16 = jnp.bfloat16
@@ -233,6 +234,7 @@
     wide_normed[...] = jnp.zeros((CELLS, WIDE), BF16)
     wide_branch[...] = jnp.zeros((CELLS, WIDE), BF16)
     tap_grad[...] = jnp.zeros_like(tap_grad)
+    rows_ud[...] = jnp.zeros_like(rows_ud)
     padded[:, 0:8, :] = jnp.zeros((ROWS, 8, C1), F32)
     padded[:, 8 + COLS :, :] = jnp.zeros((ROWS, 8, C1), F32)
     loads["table"].wait()
@@ -286,16 +288,22 @@
         for j in range(KS):
             shifted[j] = padded[:, 5 + j : 5 + j + COLS, :]
 
+    tiles = (slice(0, 128), slice(128, C1))
+
     def correlate(tap_of):
-        for r in range(ROWS):
-            total = None
-            for i in range(KS):
-                if 0 <= r + i - 3 < ROWS:
-                    for j in range(KS):
-                        tap = tap_of(i, j)
-                        term = shifted[j, r + i - 3] * taps_ref[tap : tap + 1, :]
-                        total = term if total is None else total + term
-            mixed_ref[r] = total
+        for lanes in tiles:
+            totals = [None] * ROWS
+            for j in range(KS):
+                column = [taps_ref[tap_of(i, j) : tap_of(i, j) + 1, lanes] for i in range(KS)]
+                for k in range(ROWS):
+                    values = shifted[j, k, :, lanes]
+                    for i in range(KS):
+                        r = k - i + 3
+                        if 0 <= r < ROWS:
+                            term = values * column[i]
+                            totals[r] = term if totals[r] is None else totals[r] + term
+            for r in range(ROWS):
+                mixed_ref[r, :, lanes] = totals[r]
         return mixed_ref[...].reshape(CELLS, C1)
 
     spread_columns(stem_out)
@@ -387,7 +395,9 @@
         for hi in range(NXH):
             for k in range(NY):
                 at = (hi * NY + k) * PIECE
-                blocks[at_strip, hi, k] = grads[at : at + PIECE].astype(BF16)
+                block = grads[at : at + PIECE]
+                folded = jnp.concatenate([block[0:24, 128:C1], block[24:48, 128:C1]], axis=1)
+                blocks[at_strip, hi, k] = jnp.concatenate([block[:, 0:128], folded], axis=0).astype(BF16)
 
     def core_start(*pairs):
         copies = []
@@ -412,7 +422,9 @@
         total = held[x_lo, x_hi, y].astype(F32)
         for k in range(len(plane_steps)):
             total = total + got[k].astype(F32)
-        rows[...] = total
+        rows[:, 0:128] = total[0:48]
+        rows[0:24, 128:C1] = total[48:72, 0:64]
+        rows[24:48, 128:C1] = total[48:72, 64:128]
 
     place_grads = [
         dot_nt(grad_start, ds_weight[place * C1 : (place + 1) * C1, :])[0:1] * down_gain[...]
@@ -441,15 +453,21 @@
     grad_mixed = norm_back(mixed_unit, mixed_root, grad_normed * norm1_gain[...])
 
     mixed_ref[...] = grad_mixed.reshape(ROWS, COLS, C1)
-    for i in range(KS):
+    for lanes in tiles:
+        grads = [mixed_ref[r, :, lanes] for r in range(ROWS)]
         for j in range(KS):
-            total = None
-            for r in range(ROWS):
-                if 0 <= r + i - 3 < ROWS:
-                    term = shifted[j, r + i - 3] * mixed_ref[r]
-                    total = term if total is None else total + term
-            tap = KS * i + j
-            tap_grad[tap : tap + 1, :] = jnp.sum(total, axis=0, keepdims=True)
+            totals = [None] * KS
+            for k in range(ROWS):
+                values = shifted[j, k, :, lanes]
+                for i in range(KS):
+                    r = k - i + 3
+                    if 0 <= r < ROWS:
+                        term = values * grads[r]
+                        term = (term[0:8] + term[8:16]) + (term[16:24] + term[24:32])
+                        totals[i] = term if totals[i] is None else totals[i] + term
+            for i in range(KS):
+                tap = KS * i + j
+                tap_grad[tap : tap + 1, lanes] = jnp.sum(totals[i], axis=0, keepdims=True)
 
     settle(core_ud)
     core_sum(ud, c_ud, h_ud)
@@ -532,7 +550,7 @@
     low[...] = stage[...].astype(BF16)
 
     sent = []
-    for t in range(1, NZ):
+    for t in (4, 3, 5, 2, 6, 1, 7):
         other, peer = z_peer(t)
         sent.append(ship(low_delta.at[z], low_delta.at[z], peer))
         sent.append(ship(low.at[other], got_z.at[t - 1], peer))
@@ -648,10 +666,10 @@
     plane = NX * NY
     scratch += [f32(strips, NXH, NY, 8, 128)]
     for count in (strips, NXL):
-        scratch += [bf16(count, NXH, NY, PIECE, WIDE)]
+        scratch += [bf16(count, NXH, NY, FOLDED, 128)]
         scratch += [f32(count, NXH, NY, NZ, 128), bf16(count, 24, 128)]
-    scratch += [bf16(NXL, NXH, NY, PIECE, WIDE), bf16(NXL, NXH, NY, 32, 128)]
-    scratch += [f32(plane * NC, 8, 128), bf16(plane - 1, PIECE, WIDE), bf16(plane, 32, 128)]
+    scratch += [bf16(NXL, NXH, NY, FOLDED, 128), bf16(NXL, NXH, NY, 32, 128)]
+    scratch += [f32(plane * NC, 8, 128), bf16(plane - 1, FOLDED, 128), bf16(plane, 32, 128)]
     scratch += [f32(PIECE, WIDE)] * 2 + [f32(NZ, 128)]
     scratch += [f32(NZ, 16, WIDE), bf16(NZ, 16, WIDE), bf16(NZ - 1, 16, WIDE), bf16(NZ, 24, 128)]
     scratch += [

time: 42.2 us -> 40.5 us (0.960)
  Pallas kernels: 40.7 us -> 39 us
    pallas_call x1, Pallas kernels: 39.2 us -> 37.4 us  [run_step(): pl.pallas_call(step_kernel, name='image_step_and_reduce', out_shape=(shap...]
where the time goes in v4:
time: 40.5 us; the launch traced here: 40.3 us
  Pallas kernels  39 us (96%)
  between operations  1.29 us (3%)
    pallas_call x1, Pallas kernels, run_step(): pl.pallas_call(step_kernel, name='image_step_and_reduce', out_shape=(shap...  37.4 us
    pallas_call x1, Pallas kernels, run_finish(): pl.pallas_call(finish_kernel, name='finish', out_shape=(shaped((1,), F32)...  1.56 us

profile of v4, /device:TPU:1, one launch (start us, length us, event | category | flops | bytes accessed | tf_op | source)
XLA Modules:
  0.0 40.3 jit_solution(6394521644436500270)
XLA Ops:
  1.3 37.4 %image_step_and_reduce.1 = (bf16[4,16,256]{2,1,0:T(8,128)(2,1)}, f32[8,8,128]{2,1,0:T(8,128)}) custom-call(s32[1]{0:T(128)S(6)} %copy.24.label_in, f32[384]{0:T(512)} %head_gain_in.1, bf16[4,3,8,128]{3,2,1,0:T(8,128)(2,1)} %images.1, f32[3,8,128]{2,1,0:T(8,128)} %perturbation.1, s32[16,768]{1,0:T(8,128)} %constant.2.clone.table_in, bf16[48,192]{1,0:T(8,128)(2,1)} %stem_in.1, ...), custom_call_target="tpu_custom_call" | custom-call | tf_op jit(solution)/shard_map/image_step_and_reduce/pallas_call | solution.py:680
  38.7 1.6 %finish.1 = (f32[1]{0:T(128)}, f32[3,8,128]{2,1,0:T(8,128)}, f32[3,48]{1,0:T(4,128)}, f32[3,49]{1,0:T(4,128)}, f32[12,192]{1,0:T(8,128)}, /*index=5*/f32[12,192]{1,0:T(8,128)}, f32[6,768]{1,0:T(8,128)}, f32[6,62]{1,0:T(8,128)}) custom-call(s32[3]{0:T(128)} %levels.1, bf16[4,16,256]{2,1,0:T(8,128)(2,1)} %get-tuple-element.18.shares, ...), custom_call_target="tpu_custom_call" | custom-call | tf_op jit(solution)/shard_map/finish/pallas_call | solution.py:694
